TPU v7x, 32 devices: a whole 2x2x4 slice. The times are simulated.
32 devices in a mesh: dp: 8 (over y, x, core), seq: 4 (over z).
Axes of the slice: x: 2, y: 2, z: 4, core: 2. Of those that a mesh axis runs over, the one named last changes fastest.
Arguments:
- block_input: bfloat16 [4096, 1024], P(('dp', 'seq')), may hold values from -6 to 6
- cotangent: bfloat16 [4096, 1024], P(('dp', 'seq')), may hold values from -6 to 6
- ln1_gain: bfloat16 [1024], P(('dp', 'seq')), may hold values from 0.5 to 1.5
- ln1_bias: bfloat16 [1024], P(('dp', 'seq')), may hold values from -3 to 3
- qkv_weight: bfloat16 [1024, 3072], P(('dp', 'seq')), may hold values from -0.25 to 0.25
- qv_bias: bfloat16 [2048], P(('dp', 'seq')), may hold values from -3 to 3
- out_weight: bfloat16 [1024, 1024], P(('dp', 'seq')), may hold values from -0.75 to 0.75
- out_bias: bfloat16 [1024], P(('dp', 'seq')), may hold values from -3 to 3
- ln2_gain: bfloat16 [1024], P(('dp', 'seq')), may hold values from 0.5 to 1.5
- ln2_bias: bfloat16 [1024], P(('dp', 'seq')), may hold values from -3 to 3
- fc_weight: bfloat16 [1024, 4096], P(('dp', 'seq')), may hold values from -0.1875 to 0.1875
- fc_bias: bfloat16 [4096], P(('dp', 'seq')), may hold values from -3 to 3
- proj_weight: bfloat16 [4096, 1024], P(('dp', 'seq')), may hold values from -0.09375 to 0.09375
- proj_bias: bfloat16 [1024], P(('dp', 'seq')), may hold values from -3 to 3
Outputs:
- block_output: float32 [4096, 1024], P(('dp', 'seq'))
- grad_input: float32 [4096, 1024], P(('dp', 'seq'))
- grad_ln1_gain: float32 [1024], P(('dp', 'seq'))
- grad_ln1_bias: float32 [1024], P(('dp', 'seq'))
- grad_qkv_weight: float32 [1024, 3072], P(('dp', 'seq'))
- grad_qv_bias: float32 [2048], P(('dp', 'seq'))
- grad_out_weight: float32 [1024, 1024], P(('dp', 'seq'))
- grad_out_bias: float32 [1024], P(('dp', 'seq'))
- grad_ln2_gain: float32 [1024], P(('dp', 'seq'))
- grad_ln2_bias: float32 [1024], P(('dp', 'seq'))
- grad_fc_weight: float32 [1024, 4096], P(('dp', 'seq'))
- grad_fc_bias: float32 [4096], P(('dp', 'seq'))
- grad_proj_weight: float32 [4096, 1024], P(('dp', 'seq'))
- grad_proj_bias: float32 [1024], P(('dp', 'seq'))
All inputs are finite; a program needn't handle non-finite values.
Results may differ from a plain program's by a relative error of at most 0.02.
Values may be sent and summed in bfloat16 or wider, within the bound.
A program may use at most 192 MiB of HBM per device.

v0:
```python
import math

import jax
import jax.numpy as jnp
from jax import lax
from jax.sharding import PartitionSpec as P

D = 1024
H = 16
HD = 64
FF = 4096


EPS = 1e-05
GELU_COEF = math.sqrt(2.0 / math.pi)
group_heads = 4


def layer_norm(values, norm_gain, offset):
    center = jnp.mean(values, axis=-1, keepdims=True)
    centred = values - center
    spread = jnp.mean(centred * centred, axis=-1, keepdims=True)
    return centred * lax.rsqrt(spread + EPS) * norm_gain + offset


def gelu_tanh(pre_act):
    return (
        0.5
        * pre_act
        * (1.0 + jnp.tanh(GELU_COEF * (pre_act + 0.044715 * pre_act * pre_act * pre_act)))
    )


def halved(values):
    return values.astype(jnp.bfloat16)


def widened(values):
    return values.astype(jnp.float32)


def matmul(left, right):
    return jnp.dot(left, right, preferred_element_type=jnp.float32)


def split_heads(values):
    number = values.shape[0]
    return values.reshape(number, H // group_heads, group_heads, HD).transpose(1, 2, 0, 3)


def merge_heads(values):
    number = values.shape[2]
    return values.transpose(2, 0, 1, 3).reshape(number, H * HD)


def local(
    block_input,
    cotangent,
    ln1_gain,
    ln1_bias,
    qkv_weight,
    qv_bias,
    out_weight,
    out_bias,
    ln2_gain,
    ln2_bias,
    fc_weight,
    fc_bias,
    proj_weight,
    proj_bias,
):
    score_scale = HD ** (-0.5)
    attn_full = (
        lax.all_gather(ln1_gain, ("dp", "seq"), axis=0, tiled=True),
        lax.all_gather(ln1_bias, ("dp", "seq"), axis=0, tiled=True),
        lax.all_gather(qkv_weight, ("dp", "seq"), axis=0, tiled=True),
        lax.all_gather(qv_bias, ("dp", "seq"), axis=0, tiled=True),
        lax.all_gather(out_weight, ("dp", "seq"), axis=0, tiled=True),
        lax.all_gather(out_bias, ("dp", "seq"), axis=0, tiled=True),
        lax.all_gather(ln2_gain, ("dp", "seq"), axis=0, tiled=True),
        lax.all_gather(ln2_bias, ("dp", "seq"), axis=0, tiled=True),
        lax.all_gather(proj_bias, ("dp", "seq"), axis=0, tiled=True),
    )
    (
        gain_one,
        bias_one,
        qkv_full,
        qv_full,
        out_full,
        out_bias_full,
        gain_two,
        bias_two,
        proj_bias_full,
    ) = attn_full
    stream = widened(block_input)
    tok_rows = stream.shape[0]
    normed_one = halved(layer_norm(stream, widened(gain_one), widened(bias_one)))
    projected = matmul(normed_one, qkv_full)
    queries = halved(projected[:, :D] + widened(qv_full[:D]))
    key_rows = halved(projected[:, D : 2 * D])
    value_rows = halved(projected[:, 2 * D :] + widened(qv_full[D:]))
    key_all, value_all = (
        lax.all_gather(key_rows, "seq", axis=0, tiled=True),
        lax.all_gather(value_rows, "seq", axis=0, tiled=True),
    )
    length = key_all.shape[0]
    query_pos = lax.axis_index("seq") * tok_rows + jnp.arange(tok_rows, dtype=jnp.int32)
    key_pos = jnp.arange(length, dtype=jnp.int32)
    visible = key_pos[None, :] <= query_pos[:, None]
    query_groups = split_heads(queries)
    key_groups = split_heads(key_all)
    value_groups = split_heads(value_all)

    def group_scores(query_group, key_group):
        return (
            jnp.einsum("hqd,hkd->hqk", query_group, key_group, preferred_element_type=jnp.float32)
            * score_scale
        )

    def forward_group(operands):
        query_group, key_group, value_group = operands
        scores = group_scores(query_group, key_group)
        row_total = jnp.sum(jnp.where(visible, jnp.exp(scores), 0.0), axis=-1)
        log_total = jnp.log(row_total)
        shares = halved(jnp.where(visible, jnp.exp(scores - log_total[:, :, None]), 0.0))
        mixed_heads = jnp.einsum(
            "hqk,hkd->hqd", shares, value_group, preferred_element_type=jnp.float32
        )
        return (halved(mixed_heads), log_total)

    attended_groups, log_totals = lax.map(forward_group, (query_groups, key_groups, value_groups))
    attended = merge_heads(attended_groups)
    middle = stream + matmul(attended, out_full) + widened(out_bias_full)
    normed_two = halved(layer_norm(middle, widened(gain_two), widened(bias_two)))
    grad_out = widened(cotangent)
    grad_half = halved(grad_out)
    d_proj_bias = jnp.sum(grad_out, axis=0)
    seq_count = lax.axis_size("seq")
    dp_count = lax.axis_size("dp")
    rows_own = fc_weight.shape[0]
    units_own = fc_bias.shape[0]
    fc_split = fc_weight.reshape(rows_own, dp_count, seq_count, units_own)
    fc_block = lax.all_to_all(fc_split, "seq", split_axis=2, concat_axis=0, tiled=True)
    fc_gathered, proj_rows, fc_bias_cols = (
        lax.all_gather(fc_block, "dp", axis=0, tiled=True),
        lax.all_gather(proj_weight, "dp", axis=0, tiled=True),
        lax.all_gather(fc_bias, "dp", axis=0, tiled=True),
    )
    fc_cols = fc_gathered.reshape(D, dp_count * units_own)
    normed_seq, grad_seq = (
        lax.all_gather(normed_two, "seq", axis=0, tiled=True),
        lax.all_gather(grad_half, "seq", axis=0, tiled=True),
    )
    pre_act = matmul(normed_seq, fc_cols) + widened(fc_bias_cols)
    hidden = halved(gelu_tanh(pre_act))
    ff_sum = lax.psum_scatter(
        matmul(hidden, proj_rows).astype(jnp.bfloat16), "seq", scatter_dimension=0, tiled=True
    ).astype(jnp.float32)
    output = middle + ff_sum + widened(proj_bias_full)
    d_proj_slice = matmul(hidden.T, grad_seq)
    grad_hidden = matmul(grad_seq, proj_rows.T)
    _, gelu_back = jax.vjp(gelu_tanh, pre_act)
    grad_pre = gelu_back(grad_hidden)[0]
    pre_half = halved(grad_pre)
    d_fc_slice = matmul(normed_seq.T, pre_half).reshape(D, dp_count, 1, units_own)
    d_fc_bias_slice = jnp.sum(grad_pre, axis=0)
    grad_normed_two = lax.psum_scatter(
        matmul(pre_half, fc_cols.T).astype(jnp.bfloat16), "seq", scatter_dimension=0, tiled=True
    ).astype(jnp.float32)
    fc_part, fc_bias_grad, proj_grad = (
        lax.psum_scatter(
            d_fc_slice.astype(jnp.bfloat16), "dp", scatter_dimension=0, tiled=True
        ).astype(jnp.float32),
        lax.psum_scatter(
            d_fc_bias_slice.astype(jnp.bfloat16), "dp", scatter_dimension=0, tiled=True
        ).astype(jnp.float32),
        lax.psum_scatter(
            d_proj_slice.astype(jnp.bfloat16), "dp", scatter_dimension=0, tiled=True
        ).astype(jnp.float32),
    )
    fc_grad = (
        lax.all_to_all(fc_part.astype(jnp.bfloat16), "seq", split_axis=0, concat_axis=2, tiled=True)
        .astype(fc_part.dtype)
        .reshape(rows_own, FF)
    )
    _, norm_back_two = jax.vjp(layer_norm, middle, widened(gain_two), widened(bias_two))
    mid_branch, d_ln2_gain, d_ln2_bias = norm_back_two(grad_normed_two)
    grad_middle = grad_out + mid_branch
    qkv_back, out_back = (
        lax.all_gather(qkv_weight, ("dp", "seq"), axis=0, tiled=True),
        lax.all_gather(out_weight, ("dp", "seq"), axis=0, tiled=True),
    )
    middle_half = halved(grad_middle)
    d_out_weight = matmul(attended.T, middle_half)
    d_out_bias = jnp.sum(grad_middle, axis=0)
    grad_attended = matmul(middle_half, out_back.T)
    row_delta = jnp.sum(split_heads(grad_attended) * widened(attended_groups), axis=-1)
    grad_att_groups = split_heads(halved(grad_attended))

    def backward_group(operands):
        query_group, key_group, value_group, log_total, grad_group, delta_group = operands
        scores = group_scores(query_group, key_group)
        shares = jnp.where(visible, jnp.exp(scores - log_total[:, :, None]), 0.0)
        shares_half = halved(shares)
        grad_shares = jnp.einsum(
            "hqd,hkd->hqk", grad_group, value_group, preferred_element_type=jnp.float32
        )
        grad_scores = halved(shares * (grad_shares - delta_group[:, :, None]))
        grad_q = (
            jnp.einsum("hqk,hkd->hqd", grad_scores, key_group, preferred_element_type=jnp.float32)
            * score_scale
        )
        grad_k = (
            jnp.einsum("hqk,hqd->hkd", grad_scores, query_group, preferred_element_type=jnp.float32)
            * score_scale
        )
        grad_v = jnp.einsum(
            "hqk,hqd->hkd", shares_half, grad_group, preferred_element_type=jnp.float32
        )
        return (grad_q, grad_k, grad_v)

    grad_q_groups, grad_k_groups, grad_v_groups = lax.map(
        backward_group,
        (query_groups, key_groups, value_groups, log_totals, grad_att_groups, row_delta),
    )
    grad_keys_own, grad_values_own = (
        lax.psum_scatter(
            merge_heads(grad_k_groups).astype(jnp.bfloat16), "seq", scatter_dimension=0, tiled=True
        ).astype(jnp.float32),
        lax.psum_scatter(
            merge_heads(grad_v_groups).astype(jnp.bfloat16), "seq", scatter_dimension=0, tiled=True
        ).astype(jnp.float32),
    )
    grad_queries = merge_heads(grad_q_groups)
    grad_qkv = jnp.concatenate([grad_queries, grad_keys_own, grad_values_own], axis=1)
    qkv_half = halved(grad_qkv)
    d_qkv_weight = matmul(normed_one.T, qkv_half)
    d_qv_bias = jnp.concatenate([jnp.sum(grad_queries, axis=0), jnp.sum(grad_values_own, axis=0)])
    grad_normed_one = matmul(qkv_half, qkv_back.T)
    _, norm_back_one = jax.vjp(layer_norm, stream, widened(gain_one), widened(bias_one))
    stream_branch, d_ln1_gain, d_ln1_bias = norm_back_one(grad_normed_one)
    attn_grads = (
        lax.psum_scatter(d_ln1_gain, ("dp", "seq"), scatter_dimension=0, tiled=True),
        lax.psum_scatter(d_ln1_bias, ("dp", "seq"), scatter_dimension=0, tiled=True),
        lax.psum_scatter(d_qkv_weight, ("dp", "seq"), scatter_dimension=0, tiled=True),
        lax.psum_scatter(d_qv_bias, ("dp", "seq"), scatter_dimension=0, tiled=True),
        lax.psum_scatter(d_out_weight, ("dp", "seq"), scatter_dimension=0, tiled=True),
        lax.psum_scatter(d_out_bias, ("dp", "seq"), scatter_dimension=0, tiled=True),
        lax.psum_scatter(d_ln2_gain, ("dp", "seq"), scatter_dimension=0, tiled=True),
        lax.psum_scatter(d_ln2_bias, ("dp", "seq"), scatter_dimension=0, tiled=True),
        lax.psum_scatter(d_proj_bias, ("dp", "seq"), scatter_dimension=0, tiled=True),
    )
    grad_stream = grad_middle + stream_branch
    return (
        output,
        grad_stream,
        attn_grads[0],
        attn_grads[1],
        attn_grads[2],
        attn_grads[3],
        attn_grads[4],
        attn_grads[5],
        attn_grads[6],
        attn_grads[7],
        fc_grad,
        fc_bias_grad,
        proj_grad,
        attn_grads[8],
    )


def solution(mesh):
    in_specs = (
        P(("dp", "seq"), None),
        P(("dp", "seq"), None),
        P(("dp", "seq")),
        P(("dp", "seq")),
        P(("dp", "seq"), None),
        P(("dp", "seq")),
        P(("dp", "seq"), None),
        P(("dp", "seq")),
        P(("dp", "seq")),
        P(("dp", "seq")),
        P(("dp", "seq"), None),
        P(("dp", "seq")),
        P(("dp", "seq"), None),
        P(("dp", "seq")),
    )
    out_specs = (
        P(("dp", "seq"), None),
        P(("dp", "seq"), None),
        P(("dp", "seq")),
        P(("dp", "seq")),
        P(("dp", "seq"), None),
        P(("dp", "seq")),
        P(("dp", "seq"), None),
        P(("dp", "seq")),
        P(("dp", "seq")),
        P(("dp", "seq")),
        P(("dp", "seq"), None),
        P(("dp", "seq")),
        P(("dp", "seq"), None),
        P(("dp", "seq")),
    )
    return jax.shard_map(local, mesh=mesh, in_specs=in_specs, out_specs=out_specs, check_vma=False)
```

profile of v0, /device:TPU:0, one launch (start us, length us, event | category | flops | bytes accessed | tf_op | source)
XLA Modules:
  0.0 874.3 jit_solution(2893186960389102668)
XLA Ops:
  13.8 42.5 %all-reduce.16 = (bf16[1024]{0:T(1024)(128)(2,1)S(1)}, bf16[1024]{0:T(1024)(128)(2,1)S(1)}, bf16[2048]{0:T(1024)(128)(2,1)S(1)}, bf16[1024]{0:T(1024)(128)(2,1)S...) all-reduce(bf16[1024]{0:T(1024)(128)(2,1)S(1)} %dynamic-update-slic, ...), channel_id=1, replica_groups=mesh['dp'=8,'seq'=4] {'dp','seq'}, use_global_device_ids=true, to_apply=%add.1 | all-reduce | flops 8192 | bytes 32768
  58.6 24.2 %all-gather.10.cloned.1.call-done = bf16[1024,3072]{1,0:T(8,128)(2,1)} async-done(((bf16[32,3072]{1,0:T(8,128)(2,1)}), bf16[1024,3072]{1,0:T(8,128)(2,1)}) %all-gather.10.cloned.1.call-update) | async-done | bytes 6291472 | tf_op jit(solution)/shard_map/all_gather | solution.py:76
  93.5 15.9 %all-to-all-done = bf16[32,8,4,128]{3,1,0,2:T(8,128)(2,1)S(1)} async-done(((bf16[32,8,4,128]{3,1,0,2:T(8,128)(2,1)}), bf16[32,8,4,128]{3,1,0,2:T(8,128)(2,1)S(1)}, u32[]{:S(2)}, u32[]{:S(2)}) %all-to-all-start) | async-done | bytes 262176 | tf_op jit(solution)/shard_map/all_to_all | solution.py:143
  110.4 9.8 %all-gather.12.cloned.1.call-done = bf16[512,1024]{1,0:T(8,128)(2,1)} async-done(((bf16[128,1024]{1,0:T(8,128)(2,1)}), bf16[512,1024]{1,0:T(8,128)(2,1)}) %all-gather.12.cloned.1.call-update) | async-done | bytes 1048592 | tf_op jit(solution)/shard_map/all_gather | solution.py:103
  121.6 26.9 %all-gather.14.cloned.1.call-done = bf16[512,1024]{1,0:T(8,128)(2,1)} async-done(((bf16[128,1024]{1,0:T(8,128)(2,1)}), bf16[512,1024]{1,0:T(8,128)(2,1)}) %all-gather.14.cloned.1.call-update) | async-done | bytes 1048592 | tf_op jit(solution)/shard_map/all_gather | solution.py:104
  154.4 52.6 %all-gather.16.cloned.1.call-done = bf16[1024,1024]{1,0:T(8,128)(2,1)} async-done(((bf16[32,1024]{1,0:T(8,128)(2,1)}), bf16[1024,1024]{1,0:T(8,128)(2,1)}) %all-gather.16.cloned.1.call-update) | async-done | bytes 2097168 | tf_op jit(solution)/shard_map/all_gather | solution.py:78
  211.9 9.0 %all-gather = bf16[8,1,128]{2,1,0:T(2,128)(2,1)S(1)} all-gather(bf16[1,1,128]{2,1,0:T(2,128)(2,1)S(1)} %bitcast.176), channel_id=1, replica_groups=mesh['dp'=8,'seq'=4] {'dp'}, dimensions={0}, use_global_device_ids=true | all-gather | bytes 2304 | tf_op jit(solution)/shard_map/all_gather | solution.py:147
  220.9 15.1 %all-gather.20.cloned.1.call-done = bf16[1024,8,1,128]{3,1,2,0:T(8,128)(2,1)} async-done(((bf16[128,8,1,128]{3,1,2,0:T(8,128)(2,1)}), bf16[1024,8,1,128]{3,1,2,0:T(8,128)(2,1)}) %all-gather.20.cloned.1.call-update) | async-done | bytes 2097168 | tf_op jit(solution)/shard_map/all_gather | solution.py:145
  239.3 26.8 %all-gather.18.cloned.1.call-done = bf16[512,1024]{1,0:T(8,128)(2,1)} async-done(((bf16[128,1024]{1,0:T(8,128)(2,1)}), bf16[512,1024]{1,0:T(8,128)(2,1)}) %all-gather.18.cloned.1.call-update) | async-done | bytes 1048592 | tf_op jit(solution)/shard_map/all_gather | solution.py:151
  269.9 25.1 %all-gather.24.cloned.1.call-done = bf16[512,1024]{1,0:T(8,128)(2,1)} async-done(((bf16[128,1024]{1,0:T(8,128)(2,1)}), bf16[512,1024]{1,0:T(8,128)(2,1)}) %all-gather.24.cloned.1.call-update) | async-done | bytes 1048592 | tf_op jit(solution)/shard_map/all_gather | solution.py:152
  295.0 29.1 %all-gather.22.cloned.1.call-done = bf16[1024,1024]{1,0:T(8,128)(2,1)} async-done(((bf16[128,1024]{1,0:T(8,128)(2,1)}), bf16[1024,1024]{1,0:T(8,128)(2,1)}) %all-gather.22.cloned.1.call-update) | async-done | bytes 2097168 | tf_op jit(solution)/shard_map/all_gather | solution.py:146
  324.1 5.4 fusion.91
  337.6 22.6 %reduce-scatter.15.cloned.1.call-done = bf16[128,1024]{1,0:T(8,128)(2,1)} async-done(((bf16[512,1024]{1,0:T(8,128)(2,1)}), bf16[128,1024]{1,0:T(8,128)(2,1)}) %reduce-scatter.15.cloned.1.call-update) | async-done | bytes 262160 | tf_op jit(solution)/shard_map/reduce_scatter | solution.py:167
  362.7 25.4 %reduce-scatter.13.cloned.1.call-done = bf16[128,1024]{1,0:T(8,128)(2,1)} async-done(((bf16[512,1024]{1,0:T(8,128)(2,1)}), bf16[128,1024]{1,0:T(8,128)(2,1)}) %reduce-scatter.13.cloned.1.call-update) | async-done | bytes 262160 | tf_op jit(solution)/shard_map/reduce_scatter | solution.py:156
  394.6 18.0 %while.29 = (s32[]{:T(128)}, f32[4,4,128,64]{2,3,1,0:T(8,128)}, bf16[4,4,512,64]{2,3,1,0:T(8,128)(2,1)}, bf16[4,4,512,64]{2,3,1,0:T(8,128)(2,1)}, bf16[4,4,128,6...) while((s32[]{:T(128)}, f32[4,4,128,64]{2,3,1,0:T(8,128)}, ...), condition=%wide.region_13.14_spmd.clone, body=%wide.region_12.13_spmd.clone.sunk | while | flops 169836544 | bytes 23873264 | solution.py:222
  432.2 8.7 %reduce-scatter.27.cloned.1.call-done = bf16[128,1024]{1,0:T(8,128)(2,1)} async-done(((bf16[512,1024]{1,0:T(8,128)(2,1)}), bf16[128,1024]{1,0:T(8,128)(2,1)}) %reduce-scatter.27.cloned.1.call-update) | async-done | bytes 262160
  442.0 26.9 %reduce-scatter.25.cloned.1.call-done = bf16[128,1024]{1,0:T(8,128)(2,1)} async-done(((bf16[512,1024]{1,0:T(8,128)(2,1)}), bf16[128,1024]{1,0:T(8,128)(2,1)}) %reduce-scatter.25.cloned.1.call-update) | async-done | bytes 262160
  470.0 6.5 fusion.75
  476.6 35.2 %reduce-scatter.21.cloned.1.call-done = bf16[128,8,1,128]{3,1,2,0:T(8,128)(2,1)} async-done(((bf16[1024,8,1,128]{3,1,2,0:T(8,128)(2,1)}), bf16[128,8,1,128]{3,1,2,0:T(8,128)(2,1)}) %reduce-scatter.21.cloned.1.call-update) | async-done | bytes 262160 | tf_op jit(solution)/shard_map/reduce_scatter | solution.py:171
  517.6 12.6 %all-reduce.13 = bf16[1024]{0:T(1024)(128)(2,1)S(1)} all-reduce(bf16[1024]{0:T(1024)(128)(2,1)S(1)} %get-tuple-element.216), channel_id=15, replica_groups=mesh['dp'=8,'seq'=4] {'dp'}, use_global_device_ids=true, to_apply=%region_35.36.clone | all-reduce | flops 1024 | bytes 4096
  531.1 25.0 %reduce-scatter.23.cloned.1.call-done = bf16[128,1024]{1,0:T(8,128)(2,1)} async-done(((bf16[1024,1024]{1,0:T(8,128)(2,1)}), bf16[128,1024]{1,0:T(8,128)(2,1)}) %reduce-scatter.23.cloned.1.call-update) | async-done | bytes 262160 | tf_op jit(solution)/shard_map/reduce_scatter | solution.py:177
  564.9 40.5 %all-reduce.15 = (f32[1024]{0:T(1024)S(1)}, f32[1024]{0:T(1024)S(1)}, f32[2048]{0:T(1024)S(1)}, f32[1024]{0:T(1024)S(1)}, f32[1024]{0:T(1024)S(1)}, /*index=5*/f32[1024]{0:T(1024)S(1)}, f32[1024]{0:T(1024)S(1)}) all-reduce(f32[1024]{0:T(1024)S(1)} %get-tuple-element.160, ...), channel_id=6, replica_groups=mesh['dp'=8,'seq'=4] {'dp','seq'}, use_global_device_ids=true, to_apply=%region_19.20.clone | all-reduce | flops 8192 | bytes 65536
  610.5 97.4 %reduce-scatter.19.cloned.1.call-done = f32[32,1024]{1,0:T(8,128)} async-done(((f32[1024,1024]{1,0:T(8,128)}), f32[32,1024]{1,0:T(8,128)}) %reduce-scatter.19.cloned.1.call-update) | async-done | bytes 131088 | tf_op jit(solution)/shard_map/reduce_scatter | solution.py:247
  707.9 159.9 %reduce-scatter.17.cloned.1.call-done = f32[32,3072]{1,0:T(8,128)} async-done(((f32[1024,3072]{1,0:T(8,128)}), f32[32,3072]{1,0:T(8,128)}) %reduce-scatter.17.cloned.1.call-update) | async-done | bytes 393232 | tf_op jit(solution)/shard_map/reduce_scatter | solution.py:245
  (239 shorter events, 120.2 us)
Async XLA Ops:
  7.2 75.7 %all-gather.10.cloned.1.call-start = ((), (), s32[]{:S(2)}) async-start(), calls=%async_computation.10 | async-start | bytes 6488064 | tf_op jit(solution)/shard_map/all_gather | solution.py:76
  7.9 112.2 %all-gather.12.cloned.1.call-start = ((), (), s32[]{:S(2)}) async-start(), calls=%async_computation.11 | async-start | bytes 1310720 | tf_op jit(solution)/shard_map/all_gather | solution.py:103
  87.6 60.9 %all-gather.14.cloned.1.call-start = ((), (), s32[]{:S(2)}) async-start(), calls=%async_computation.12 | async-start | bytes 1310720 | tf_op jit(solution)/shard_map/all_gather | solution.py:104
  88.5 118.6 %all-gather.16.cloned.1.call-start = ((), (), s32[]{:S(2)}) async-start(), calls=%async_computation.13 | async-start | bytes 2162688 | tf_op jit(solution)/shard_map/all_gather | solution.py:78
  90.0 19.4 %all-to-all-start = ((bf16[32,8,4,128]{3,1,0,2:T(8,128)(2,1)}), bf16[32,8,4,128]{3,1,0,2:T(8,128)(2,1)S(1)}, u32[]{:S(2)}, u32[]{:S(2)}) async-start(bf16[32,8,4,128]{3,1,0,2:T(8,128)(2,1)} %copy.53), calls=%async_computation | async-start | bytes 524288 | tf_op jit(solution)/shard_map/all_to_all | solution.py:143
  93.4 142.6 %all-gather.20.cloned.1.call-start = ((), (), s32[]{:S(2)}) async-start(), calls=%async_computation.15 | async-start | bytes 2359296 | tf_op jit(solution)/shard_map/all_gather | solution.py:145
  110.1 155.9 %all-gather.18.cloned.1.call-start = ((), (), s32[]{:S(2)}) async-start(), calls=%async_computation.14 | async-start | bytes 1310720 | tf_op jit(solution)/shard_map/all_gather | solution.py:151
  150.0 57.1 %copy-start = (bf16[128,1024]{1,0:T(8,128)(2,1)S(1)}, bf16[128,1024]{1,0:T(8,128)(2,1)}, u32[]{:S(2)}) copy-start(bf16[128,1024]{1,0:T(8,128)(2,1)} %param.18) | copy-start | bytes 786436
  154.4 52.7 %copy-start.8 = (bf16[4,4,128,64]{2,3,1,0:T(8,128)(2,1)}, bf16[4,4,128,64]{2,3,1,0:T(8,128)(2,1)S(1)}, u32[]{:S(2)}) copy-start(bf16[4,4,128,64]{2,3,1,0:T(8,128)(2,1)S(1)} %get-tuple-element.449) | copy-start | bytes 786436
  154.4 55.9 %copy-start.2 = (bf16[4,4,512,64]{2,3,1,0:T(8,128)(2,1)}, bf16[4,4,512,64]{2,3,1,0:T(8,128)(2,1)S(1)}, u32[]{:S(2)}) copy-start(bf16[4,4,512,64]{2,3,1,0:T(8,128)(2,1)S(1)} %get-tuple-element.439) | copy-start | bytes 3145732
  154.4 55.9 %copy-start.4 = (bf16[4,4,512,64]{2,3,1,0:T(8,128)(2,1)}, bf16[4,4,512,64]{2,3,1,0:T(8,128)(2,1)S(1)}, u32[]{:S(2)}) copy-start(bf16[4,4,512,64]{2,3,1,0:T(8,128)(2,1)S(1)} %get-tuple-element.440) | copy-start | bytes 3145732
  154.4 55.9 %copy-start.5 = (bf16[4,4,128,64]{2,3,1,0:T(8,128)(2,1)}, bf16[4,4,128,64]{2,3,1,0:T(8,128)(2,1)S(1)}, u32[]{:S(2)}) copy-start(bf16[4,4,128,64]{2,3,1,0:T(8,128)(2,1)S(1)} %get-tuple-element.111) | copy-start | bytes 786436
  210.4 84.6 %all-gather.24.cloned.1.call-start = ((), (), s32[]{:S(2)}) async-start(), calls=%async_computation.18 | async-start | bytes 1310720 | tf_op jit(solution)/shard_map/all_gather | solution.py:152
  211.1 113.0 %all-gather.22.cloned.1.call-start = ((), (), s32[]{:S(2)}) async-start(), calls=%async_computation.16 | async-start | bytes 2359296 | tf_op jit(solution)/shard_map/all_gather | solution.py:146
  211.9 148.3 %reduce-scatter.15.cloned.1.call-start = ((), (), s32[]{:S(2)}) async-start(), calls=%async_computation.19 | async-start | bytes 1310720 | tf_op jit(solution)/shard_map/reduce_scatter | solution.py:167
  332.7 55.4 %reduce-scatter.13.cloned.1.call-start = ((), (), s32[]{:S(2)}) async-start(), calls=%async_computation.17 | async-start | bytes 1310720 | tf_op jit(solution)/shard_map/reduce_scatter | solution.py:156
  337.5 52.8 %copy-start.1 = (bf16[1024,1024]{1,0:T(8,128)(2,1)S(1)}, bf16[1024,1024]{1,0:T(8,128)(2,1)}, u32[]{:S(2)}) copy-start(bf16[1024,1024]{1,0:T(8,128)(2,1)} %all-gather.16.cloned.1.call-done) | copy-start | bytes 6291460
  337.5 103.4 %reduce-scatter.27.cloned.1.call-start = ((), (), s32[]{:S(2)}) async-start(), calls=%async_computation.25 | async-start | bytes 1310720
  415.0 53.9 %reduce-scatter.25.cloned.1.call-start = ((), (), s32[]{:S(2)}) async-start(), calls=%async_computation.24 | async-start | bytes 1310720
  416.4 95.4 %reduce-scatter.21.cloned.1.call-start = ((), (), s32[]{:S(2)}) async-start(), calls=%async_computation.22 | async-start | bytes 2359296 | tf_op jit(solution)/shard_map/reduce_scatter | solution.py:171
  422.5 133.6 %reduce-scatter.23.cloned.1.call-start = ((), (), s32[]{:S(2)}) async-start(), calls=%async_computation.23 | async-start | bytes 2359296 | tf_op jit(solution)/shard_map/reduce_scatter | solution.py:177
  428.3 279.6 %reduce-scatter.19.cloned.1.call-start = ((), (), s32[]{:S(2)}) async-start(), calls=%async_computation.21 | async-start | bytes 4325376 | tf_op jit(solution)/shard_map/reduce_scatter | solution.py:247
  431.1 436.7 %reduce-scatter.17.cloned.1.call-start = ((), (), s32[]{:S(2)}) async-start(), calls=%async_computation.20 | async-start | bytes 12976128 | tf_op jit(solution)/shard_map/reduce_scatter | solution.py:245
  511.8 46.1 %all-to-all-start.1 = ((bf16[128,8,1,128]{3,1,2,0:T(8,128)(2,1)}), bf16[128,8,1,128]{3,1,2,0:T(8,128)(2,1)S(1)}, u32[]{:S(2)}, u32[]{:S(2)}) async-start(bf16[128,8,1,128]{3,1,2,0:T(8,128)(2,1)} %reduce-scatter.21.cloned.1.call-done), calls=%async_computation.6 | async-start | bytes 524288 | tf_op jit(solution)/shard_map/all_to_all | solution.py:182
  (27 other events, 92.7 us)
Sparse Core Ops, SparseCore 0:
  10.9 71.9 all-gather.9
  87.7 32.3 all-gather.11
  122.3 26.1 all-gather.13
  151.3 55.7 all-gather.15
  209.4 26.6 all-gather.19
  238.0 27.9 all-gather.17
  267.6 27.3 all-gather.23
  296.9 27.1 all-gather.21
  332.8 27.2 reduce-scatter.14
  362.3 25.7 reduce-scatter.12
  415.1 25.7 reduce-scatter.26
  443.1 25.7 reduce-scatter.24
  472.2 39.5 reduce-scatter.20
  514.9 41.0 reduce-scatter.22
  558.8 149.0 reduce-scatter.18
  714.3 153.4 reduce-scatter.16
where the time goes:
time: 876 us; the launch traced here: 874 us
  waiting for transfers between devices  629 us (72%)
  blocking collectives  105 us (12%)
  matrix products  62.5 us (7%)
  local copies, waits for them, and re-layouts  39.6 us (5%)
  between operations  15 us (2%)
  other arithmetic  14 us (2%)
  starting transfers between devices  8.88 us (1%)
    reduce_scatter x1, waiting for transfers between devices, local(): lax.psum_scatter(d_qkv_weight, ('dp', 'seq'), scatter_dimension=0, tiled=...  160 us
    reduce_scatter x1, waiting for transfers between devices, local(): lax.psum_scatter(d_out_weight, ('dp', 'seq'), scatter_dimension=0, tiled=...  97.4 us
    unnamed x3, blocking collectives  95.5 us
    all_gather x1, waiting for transfers between devices, local(): lax.all_gather(out_weight, ('dp', 'seq'), axis=0, tiled=True)  52.6 us
    dot_general x12, matrix products, matmul(): return jnp.dot(left, right, preferred_element_type=jnp.float32)  45.8 us
    unnamed x18, waiting for transfers between devices  38.4 us
    reduce_scatter x1, waiting for transfers between devices, local(): lax.psum_scatter(d_fc_slice.astype(jnp.bfloat16), 'dp', scatter_dimension...  35.2 us
    all_gather x1, waiting for transfers between devices, local(): lax.all_gather(proj_weight, 'dp', axis=0, tiled=True)  29.1 us
  transfers between devices with their start and end apart: 18, of which 17 were waited for; matrix products, arithmetic and copies ran while one was open for 8% of the time, Pallas kernels for 0%

commit v1 on v0

v1 whole, which is shorter than its diff:
```python
import math

import jax
import jax.numpy as jnp
from jax import lax
from jax.experimental import pallas as pl
from jax.experimental.pallas import tpu as pltpu
from jax.sharding import PartitionSpec as P

D = 1024
H = 16
HD = 64
FF = 4096


EPS = 1e-05
GELU_COEF = math.sqrt(2.0 / math.pi)
MESH = pl.DeviceIdType.MESH


def layer_norm(values, norm_gain, offset):
    center = jnp.mean(values, axis=-1, keepdims=True)
    centred = values - center
    spread = jnp.mean(centred * centred, axis=-1, keepdims=True)
    return centred * lax.rsqrt(spread + EPS) * norm_gain + offset


def gelu_tanh(pre_act):
    return (
        0.5
        * pre_act
        * (1.0 + jnp.tanh(GELU_COEF * (pre_act + 0.044715 * pre_act * pre_act * pre_act)))
    )


def halved(values):
    return values.astype(jnp.bfloat16)


def widened(values):
    return values.astype(jnp.float32)


def matmul(left, right):
    return jnp.dot(left, right, preferred_element_type=jnp.float32)


def place():
    return lax.axis_index("dp"), lax.axis_index("seq")


def counts():
    return lax.axis_size("dp"), lax.axis_size("seq")


def remote(src, dst, send, recv, device):
    return pltpu.make_async_remote_copy(
        src_ref=src, dst_ref=dst, send_sem=send, recv_sem=recv, device_id=device, device_id_type=MESH
    )


def dma(*shape):
    return pltpu.SemaphoreType.DMA(shape)


def greet_all():
    dp, s = place()
    dpc, n = counts()
    barrier = pltpu.get_barrier_semaphore()

    def greet(i, carry):
        @pl.when(i != dp * n + s)
        def _():
            pl.semaphore_signal(barrier, inc=1, device_id=(i // n, i % n), device_id_type=MESH)

        return carry

    lax.fori_loop(0, dpc * n, greet, 0)
    pl.semaphore_wait(barrier, dpc * n - 1)


def greet_near():
    dp, s = place()
    dpc, n = counts()
    nc = dpc // 2
    barrier = pltpu.get_barrier_semaphore()
    for k in range(1, n):
        pl.semaphore_signal(barrier, inc=1, device_id=(dp, (s + k) % n), device_id_type=MESH)
    for k in range(1, nc):
        pl.semaphore_signal(barrier, inc=1, device_id=((dp + 2 * k) % dpc, s), device_id_type=MESH)
    pl.semaphore_signal(barrier, inc=1, device_id=(other_core(dp), s), device_id_type=MESH)
    pl.semaphore_wait(barrier, n - 1 + nc)


def greet_seq():
    dp, s = place()
    _, n = counts()
    barrier = pltpu.get_barrier_semaphore()
    for k in range(1, n):
        pl.semaphore_signal(barrier, inc=1, device_id=(dp, (s + k) % n), device_id_type=MESH)
    pl.semaphore_wait(barrier, n - 1)


def other_core(dp):
    return dp + 1 - 2 * (dp % 2)


class Exchange:
    def __init__(self, value):
        _, n = counts()
        self.operands = (value,)
        self.outs = (value,)
        self.sems = (dma(n), dma(n))

    def copies(self, ins, outs, sems):
        dp, s = place()
        _, n = counts()
        return [
            remote(
                ins[0].at[(s + k) % n], outs[0].at[s], sems[0].at[k], sems[1].at[k], (dp, (s + k) % n)
            )
            for k in range(n - 1, 0, -1)
        ]

    def start(self, ins, outs, sems):
        for copy in self.copies(ins, outs, sems):
            copy.start()

    def finish(self, ins, outs, sems):
        for copy in self.copies(ins, outs, sems):
            copy.wait()


class Plane(Exchange):
    def __init__(self, value):
        dpc, _ = counts()
        self.operands = (value,)
        self.outs = (value,)
        self.sems = (dma(dpc // 2), dma(dpc // 2))

    def copies(self, ins, outs, sems):
        dp, s = place()
        dpc, _ = counts()
        chip, core, nc = dp // 2, dp % 2, dpc // 2
        return [
            remote(
                ins[0].at[(chip + k) % nc],
                outs[0].at[chip],
                sems[0].at[k],
                sems[1].at[k],
                ((chip + k) % nc * 2 + core, s),
            )
            for k in range(1, nc)
        ]


class Partner(Exchange):
    def __init__(self, value):
        self.operands = (value,)
        self.outs = (jax.ShapeDtypeStruct(value.shape[1:], value.dtype),)
        self.sems = (dma(1), dma(1))

    def copies(self, ins, outs, sems):
        dp, s = place()
        return [
            remote(
                ins[0].at[1 - dp % 2], outs[0], sems[0].at[0], sems[1].at[0], (other_core(dp), s)
            )
        ]


class Everyone:
    def __init__(self, value):
        dpc, n = counts()
        self.operands = (value,)
        self.outs = (value,)
        self.sems = (dma(dpc * n), dma(dpc * n))

    def copy(self, ins, outs, sems, k):
        dp, s = place()
        dpc, n = counts()
        me = dp * n + s
        peer = (me + k) % (dpc * n)
        return remote(
            ins[0].at[peer], outs[0].at[me], sems[0].at[k], sems[1].at[k], (peer // n, peer % n)
        )

    def start(self, ins, outs, sems):
        def step(k, carry):
            self.copy(ins, outs, sems, k).start()
            return carry

        lax.fori_loop(1, self.outs[0].shape[0], step, 0)

    def finish(self, ins, outs, sems):
        def step(k, carry):
            self.copy(ins, outs, sems, k).wait()
            return carry

        lax.fori_loop(1, self.outs[0].shape[0], step, 0)


class Line:
    def __init__(self, value):
        _, n = counts()
        self.operands = (value,)
        self.outs = (jax.ShapeDtypeStruct((n,) + value.shape, value.dtype),)
        self.sems = (dma(2, n), dma(2, n), dma(1))

    def hand_on(self, ins, outs, sems, way, k):
        dp, s = place()
        sign = 1 - 2 * way
        block = outs[0].at[s - sign * k]
        return remote(
            ins[0] if k == 0 else block, block, sems[0].at[way, k], sems[1].at[way, k], (dp, s + sign)
        )

    def guard(self, way, k):
        _, s = place()
        _, n = counts()
        return (s >= k) if way == 0 else (s < n - k)

    def start(self, ins, outs, sems):
        _, s = place()
        _, n = counts()
        pltpu.make_async_copy(ins[0], outs[0].at[s], sems[2].at[0]).start()
        for way in (0, 1):
            follows = (s < n - 1) if way == 0 else (s > 0)

            @pl.when(follows)
            def _():
                self.hand_on(ins, outs, sems, way, 0).start()

    def step(self, ins, outs, sems, k):
        dp, s = place()
        _, n = counts()
        for way in (0, 1):
            sign = 1 - 2 * way
            follows = (s < n - 1) if way == 0 else (s > 0)

            @pl.when(self.guard(way, k))
            def _():
                block = outs[0].at[s - sign * k]
                remote(
                    block, block, sems[0].at[way, k - 1], sems[1].at[way, k - 1], (dp, s - sign)
                ).wait_recv()
                if k < n - 1:

                    @pl.when(follows)
                    def _():
                        self.hand_on(ins, outs, sems, way, k).start()

    def close(self, ins, outs, sems):
        _, s = place()
        _, n = counts()
        for way in (0, 1):
            follows = (s < n - 1) if way == 0 else (s > 0)
            for k in range(n - 1):

                @pl.when(jnp.logical_and(follows, self.guard(way, k)))
                def _():
                    self.hand_on(ins, outs, sems, way, k).wait_send()

        pltpu.make_async_copy(ins[0], outs[0].at[s], sems[2].at[0]).wait()

    def finish(self, ins, outs, sems):
        _, n = counts()
        for k in range(1, n):
            self.step(ins, outs, sems, k)
        self.close(ins, outs, sems)


class Turn:
    def __init__(self, value, outward):
        self.outward = outward
        self.operands = (value,)
        self.outs = (value,)
        self.sems = (dma(1), dma(1), dma(1))

    def target(self):
        dp, s = place()
        dpc, n = counts()
        if self.outward:
            rank = s * dpc + dp
            return rank // n, rank % n
        rank = dp * n + s
        return rank % dpc, rank // dpc

    def away(self):
        dp, s = place()
        to_dp, to_s = self.target()
        return jnp.logical_or(to_dp != dp, to_s != s)

    def copy(self, ins, outs, sems):
        return remote(ins[0], outs[0], sems[0].at[0], sems[1].at[0], self.target())

    def start(self, ins, outs, sems):
        @pl.when(self.away())
        def _():
            self.copy(ins, outs, sems).start()

        @pl.when(jnp.logical_not(self.away()))
        def _():
            pltpu.make_async_copy(ins[0], outs[0], sems[2].at[0]).start()

    def finish(self, ins, outs, sems):
        @pl.when(self.away())
        def _():
            self.copy(ins, outs, sems).wait()

        @pl.when(jnp.logical_not(self.away()))
        def _():
            pltpu.make_async_copy(ins[0], outs[0], sems[2].at[0]).wait()


def run(number, greet, *tasks):
    spans = []
    a = b = c = 0
    for task in tasks:
        spans.append((a, b, c))
        a += len(task.operands)
        b += len(task.outs)
        c += len(task.sems)
    n_in, n_out = a, b

    def kernel(*refs):
        ins, outs, sems = refs[:n_in], refs[n_in : n_in + n_out], refs[n_in + n_out :]
        greet()
        views = [
            (
                ins[i : i + len(t.operands)],
                outs[o : o + len(t.outs)],
                sems[m : m + len(t.sems)],
            )
            for t, (i, o, m) in zip(tasks, spans)
        ]
        for t, view in zip(tasks, views):
            t.start(*view)
        for t, view in zip(tasks, views):
            t.finish(*view)

    return pl.pallas_call(
        kernel,
        out_shape=[jax.ShapeDtypeStruct(o.shape, o.dtype) for t in tasks for o in t.outs],
        in_specs=[pl.BlockSpec(memory_space=pl.ANY)] * n_in,
        out_specs=[pl.BlockSpec(memory_space=pl.ANY)] * n_out,
        scratch_shapes=[s for t in tasks for s in t.sems],
        compiler_params=pltpu.CompilerParams(collective_id=number, has_side_effects=True),
    )(*[v for t in tasks for v in t.operands])


def gather_inputs(block_input, cotangent, pack, out_rows, proj_rows):
    dpc, n = counts()
    nc = dpc // 2
    tokens, grads = Line(block_input), Line(cotangent)

    def kernel(
        x_in, g_in, pack_in, out_in, proj_in, x_all, g_all, pack_all, out_all, proj_all,
        x_send, x_recv, x_own, g_send, g_recv, g_own, turn_send, turn_recv, local,
        z_send, z_recv, c_send, c_recv, p_send, p_recv,
    ):
        dp, s = place()
        chip, core = dp // 2, dp % 2
        greet_all()
        gathered = (proj_all, out_all, pack_all)
        rank = dp * n + s
        to_dp, to_s = rank % dpc, rank // dpc
        home = jnp.logical_and(to_dp == dp, to_s == s)
        turn = remote(
            out_in, out_all.at[to_dp], turn_send.at[0], turn_recv.at[0], (to_dp, to_s)
        )
        keep_out = pltpu.make_async_copy(out_in, out_all.at[dp], local.at[1])
        keep_pack = pltpu.make_async_copy(pack_in.at[s], pack_all.at[dp, s], local.at[2])
        keep_proj = pltpu.make_async_copy(proj_in, proj_all.at[dp], local.at[0])
        keep_pack.start()
        shuffles = [
            remote(
                pack_in.at[(s + k) % n], pack_all.at[dp, s], z_send.at[k], z_recv.at[k],
                (dp, (s + k) % n),
            )
            for k in range(n - 1, 0, -1)
        ]
        for copy in shuffles:
            copy.start()

        @pl.when(home)
        def _():
            keep_out.start()

        @pl.when(jnp.logical_not(home))
        def _():
            turn.start()

        keep_proj.start()

        def to_chips(a, source):
            return [
                remote(
                    source, gathered[a].at[dp], c_send.at[a, k], c_recv.at[a, k],
                    ((chip + k) % nc * 2 + core, s),
                )
                for k in range(1, nc)
            ]

        def to_partner(a, k, source):
            slot = (chip - k + nc) % nc * 2 + core
            return remote(
                source if source is not None else gathered[a].at[slot],
                gathered[a].at[slot], p_send.at[a, k], p_recv.at[a, k], (other_core(dp), s),
            )

        def arrive(a, k):
            block = gathered[a].at[(chip - k + nc) % nc * 2 + core]
            remote(
                block, block, c_send.at[a, k], c_recv.at[a, k], ((chip - k + nc) % nc * 2 + core, s)
            ).wait_recv()

        sources = (proj_in, out_all.at[dp], pack_all.at[dp])
        tokens.start((x_in,), (x_all,), (x_send, x_recv, x_own))
        for copy in to_chips(0, sources[0]):
            copy.start()
        to_partner(0, 0, sources[0]).start()

        @pl.when(home)
        def _():
            keep_out.wait()

        @pl.when(jnp.logical_not(home))
        def _():
            turn.wait()

        keep_pack.wait()
        for copy in shuffles:
            copy.wait()
        for a in (1, 2):
            for copy in to_chips(a, sources[a]):
                copy.start()
            to_partner(a, 0, sources[a]).start()
        for k in range(1, n):
            tokens.step((x_in,), (x_all,), (x_send, x_recv, x_own), k)
            if k == 1:
                grads.start((g_in,), (g_all,), (g_send, g_recv, g_own))
        for a in range(3):
            for k in range(1, nc):
                arrive(a, k)
                to_partner(a, k, None).start()
        for k in range(1, n):
            grads.step((g_in,), (g_all,), (g_send, g_recv, g_own), k)
        tokens.close((x_in,), (x_all,), (x_send, x_recv, x_own))
        grads.close((g_in,), (g_all,), (g_send, g_recv, g_own))
        for a in range(3):
            for copy in to_chips(a, sources[a]):
                copy.wait_send()
            for k in range(nc):
                slot = (chip - k + nc) % nc * 2 + 1 - core
                to_partner(a, k, sources[a] if k == 0 else None).wait_send()
                block = gathered[a].at[slot]
                remote(
                    block, block, p_send.at[a, k], p_recv.at[a, k], (other_core(dp), s)
                ).wait_recv()
        keep_proj.wait()

    def grown(value, *lead):
        return jax.ShapeDtypeStruct(lead + value.shape, value.dtype)

    return pl.pallas_call(
        kernel,
        out_shape=[
            grown(block_input, n), grown(cotangent, n), grown(pack, dpc), grown(out_rows, dpc),
            grown(proj_rows, dpc),
        ],
        in_specs=[pl.BlockSpec(memory_space=pl.ANY)] * 5,
        out_specs=[pl.BlockSpec(memory_space=pl.ANY)] * 5,
        scratch_shapes=[
            *tokens.sems, *grads.sems, dma(1), dma(1), dma(3),
            dma(n), dma(n), dma(3, nc), dma(3, nc), dma(3, nc), dma(3, nc),
        ],
        compiler_params=pltpu.CompilerParams(collective_id=0, has_side_effects=True),
    )(block_input, cotangent, pack, out_rows, proj_rows)


def total(own, received, mine):
    picked = [
        jnp.where(k == mine, widened(own[k]), widened(received[k])) for k in range(own.shape[0])
    ]
    result = picked[0]
    for value in picked[1:]:
        result = result + value
    return result


def fill(own, received, mine):
    slots = lax.broadcasted_iota(jnp.int32, (own.shape[0],) + (1,) * (own.ndim - 1), 0)
    return jnp.where(slots == mine, own, received)


def local(
    block_input,
    cotangent,
    ln1_gain,
    ln1_bias,
    qkv_weight,
    qv_bias,
    out_weight,
    out_bias,
    ln2_gain,
    ln2_bias,
    fc_weight,
    fc_bias,
    proj_weight,
    proj_bias,
):
    dp, s = place()
    dpc, n = counts()
    nc, ranks = dpc // 2, dpc * n
    core, chip = dp % 2, dp // 2
    tok_rows = block_input.shape[0]
    rows = qkv_weight.shape[0]
    units = fc_bias.shape[0]
    heads = H // n
    wide = heads * HD
    length = n * tok_rows
    score_scale = HD ** (-0.5)

    small = jnp.concatenate(
        [ln1_gain, ln1_bias, out_bias, ln2_gain, ln2_bias, proj_bias, qv_bias, fc_bias]
    )
    margin = -(-small.shape[0] // (rows * 128)) * 128
    block = jnp.pad(small, (0, rows * margin - small.shape[0])).reshape(rows, margin)
    pack = jnp.concatenate(
        [
            qkv_weight.reshape(rows, 3, n, wide).transpose(2, 0, 1, 3).reshape(n, rows, 3 * wide),
            fc_weight.reshape(rows, dpc, n, units).transpose(2, 0, 1, 3).reshape(n, rows, dpc * units),
            jnp.broadcast_to(block[None], (n, rows, margin)),
        ],
        axis=2,
    )
    x_all, g_all, pack_all, out_all, proj_all = gather_inputs(
        block_input, cotangent, pack, out_weight, proj_weight
    )
    stream_seq = widened(x_all.reshape(length, D))
    grad_seq = g_all.reshape(length, D)
    pack_rows = pack_all.reshape(D, pack.shape[2])
    qkv_cols = pack_rows[:, : 3 * wide]
    fc_cols = pack_rows[:, 3 * wide : 3 * wide + dpc * units]
    out_rows = out_all.reshape(wide, D)
    proj_rows = proj_all.reshape(dpc * units, D)
    smalls = pack_rows[:, 3 * wide + dpc * units :].reshape(ranks, rows * margin)
    gain_one, bias_one, out_bias_full, gain_two, bias_two, proj_bias_full = (
        widened(smalls[:, i * rows : (i + 1) * rows].reshape(D)) for i in range(6)
    )
    at = 6 * rows
    qv_full = smalls[:, at : at + qv_bias.shape[0]].reshape(2, n, wide)
    qv_own = widened(lax.dynamic_index_in_dim(qv_full, s, 1, keepdims=False))
    at += qv_bias.shape[0]
    fc_bias_cols = widened(
        lax.dynamic_index_in_dim(
            smalls[:, at : at + units].reshape(dpc, n, units), s, 1, keepdims=False
        ).reshape(dpc * units)
    )

    normed_one = halved(layer_norm(stream_seq, gain_one, bias_one))
    projected = matmul(normed_one, qkv_cols)

    def by_head(values):
        return values.reshape(length, heads, HD).transpose(1, 0, 2)

    def by_token(values):
        return values.transpose(1, 0, 2).reshape(length, wide)

    queries = by_head(halved(projected[:, :wide] + qv_own[0]))
    keys = by_head(halved(projected[:, wide : 2 * wide]))
    values = by_head(halved(projected[:, 2 * wide :] + qv_own[1]))
    position = jnp.arange(length, dtype=jnp.int32)
    visible = position[None, :] <= position[:, None]
    scores = (
        jnp.einsum("hqd,hkd->hqk", queries, keys, preferred_element_type=jnp.float32) * score_scale
    )
    log_total = jnp.log(
        jnp.sum(jnp.where(visible, jnp.exp(scores), 0.0), axis=-1, keepdims=True)
    )
    probs = jnp.where(visible, jnp.exp(scores - log_total), 0.0)
    shares = halved(probs)
    attended_heads = halved(
        jnp.einsum("hqk,hkd->hqd", shares, values, preferred_element_type=jnp.float32)
    )
    attended = by_token(attended_heads)
    mixed = halved(matmul(attended, out_rows)).reshape(n, tok_rows, D)
    (mixed_got,) = run(1, greet_seq, Exchange(mixed))
    stream = widened(block_input)
    middle = stream + total(mixed, mixed_got, s) + out_bias_full
    normed_two = halved(layer_norm(middle, gain_two, bias_two))
    (normed_all,) = run(2, greet_seq, Line(normed_two))
    normed_seq = normed_all.reshape(length, D)
    grad_out = widened(cotangent)
    d_proj_bias = jnp.sum(grad_out, axis=0)
    pre_act = matmul(normed_seq, fc_cols) + fc_bias_cols
    hidden = halved(gelu_tanh(pre_act))
    grad_hidden = matmul(grad_seq, proj_rows.T)
    _, gelu_back = jax.vjp(gelu_tanh, pre_act)
    grad_pre = gelu_back(grad_hidden)[0]
    pre_half = halved(grad_pre)
    back_two = halved(matmul(pre_half, fc_cols.T)).reshape(n, tok_rows, D)
    (back_two_got,) = run(3, greet_seq, Exchange(back_two))
    ff_part = halved(matmul(hidden, proj_rows)).reshape(n, tok_rows, D)

    def by_core(values):
        return halved(values).reshape(nc, 2, -1, values.shape[-1]).transpose(1, 0, 2, 3)

    d_proj = by_core(matmul(hidden.T, grad_seq))
    d_fc = by_core(matmul(normed_seq.T, pre_half))
    d_fc_bias = jnp.sum(grad_pre, axis=0).reshape(dpc, 1, units)
    _, norm_back_two = jax.vjp(layer_norm, middle, gain_two, bias_two)
    mid_branch, d_ln2_gain, d_ln2_bias = norm_back_two(total(back_two, back_two_got, s))
    grad_middle = grad_out + mid_branch
    d_out_bias = jnp.sum(grad_middle, axis=0)
    middle_all, d_proj_got, d_fc_got = run(
        4, greet_near, Line(halved(grad_middle)), Partner(d_proj), Partner(d_fc)
    )

    def pair(own, received):
        kept = lax.dynamic_index_in_dim(own, core, 0, keepdims=False)
        return halved(widened(kept) + widened(received))

    d_proj, d_fc = pair(d_proj, d_proj_got), pair(d_fc, d_fc_got)
    middle_half = middle_all.reshape(length, D)
    d_out = by_core(matmul(attended.T, middle_half))
    grad_attended = matmul(middle_half, out_rows.T)
    grad_att = by_head(halved(grad_attended))
    row_delta = jnp.sum(by_head(grad_attended) * widened(attended_heads), axis=-1, keepdims=True)
    grad_shares = jnp.einsum("hqd,hkd->hqk", grad_att, values, preferred_element_type=jnp.float32)
    grad_scores = halved(probs * (grad_shares - row_delta))
    grad_q = (
        jnp.einsum("hqk,hkd->hqd", grad_scores, keys, preferred_element_type=jnp.float32)
        * score_scale
    )
    grad_k = (
        jnp.einsum("hqk,hqd->hkd", grad_scores, queries, preferred_element_type=jnp.float32)
        * score_scale
    )
    grad_v = jnp.einsum("hqk,hqd->hkd", shares, grad_att, preferred_element_type=jnp.float32)
    grad_qkv = jnp.concatenate([by_token(grad_q), by_token(grad_k), by_token(grad_v)], axis=1)
    qkv_half = halved(grad_qkv)
    back_one = halved(matmul(qkv_half, qkv_cols.T)).reshape(n, tok_rows, D)
    d_qkv = by_core(matmul(normed_one.T, qkv_half))
    sums = jnp.sum(grad_qkv, axis=0)
    d_qv = jnp.stack([sums[:wide], sums[2 * wide :]])[:, None]
    back_one_got, d_proj_parts, d_fc_parts, d_qkv_got, d_out_got = run(
        5, greet_near, Exchange(back_one), Plane(d_proj), Plane(d_fc), Partner(d_qkv), Partner(d_out)
    )
    proj_grad = total(d_proj, d_proj_parts, chip)
    fc_rows = halved(total(d_fc, d_fc_parts, chip)).reshape(n, rows, dpc * units)
    d_qkv, d_out = pair(d_qkv, d_qkv_got), pair(d_out, d_out_got)
    _, norm_back_one = jax.vjp(layer_norm, stream, gain_one, bias_one)
    stream_branch, d_ln1_gain, d_ln1_bias = norm_back_one(total(back_one, back_one_got, s))
    grad_stream = grad_middle + stream_branch
    turn = jnp.arange(n, dtype=jnp.int32)[None, :, None] == s
    vectors = jnp.concatenate(
        [
            v.reshape(ranks, rows)
            for v in (d_ln1_gain, d_ln1_bias, d_out_bias, d_ln2_gain, d_ln2_bias, d_proj_bias)
        ]
        + [
            jnp.where(turn, d_qv, 0.0).reshape(ranks, -1),
            jnp.where(turn, d_fc_bias, 0.0).reshape(ranks, units),
        ],
        axis=1,
    )
    used = vectors.shape[1]
    vectors = jnp.pad(vectors, ((0, 0), (0, -used % 128))).reshape(ranks, -1, 128)
    d_qkv_parts, d_out_parts, fc_got, vectors_got, ff_got = run(
        6, greet_all, Plane(d_qkv), Plane(d_out), Exchange(fc_rows), Everyone(vectors), Exchange(ff_part)
    )
    output = middle + total(ff_part, ff_got, s) + proj_bias_full
    fc_grad = (
        widened(fill(fc_rows, fc_got, s))
        .reshape(n, rows, dpc, units)
        .transpose(1, 2, 0, 3)
        .reshape(rows, FF)
    )
    qkv_rows = halved(total(d_qkv, d_qkv_parts, chip)).reshape(n, rows, 3 * wide)
    out_grad_rows = halved(total(d_out, d_out_parts, chip))
    vector = jnp.sum(fill(vectors, vectors_got, dp * n + s), axis=0).reshape(-1)
    firsts = [vector[i * rows : (i + 1) * rows] for i in range(6)]
    at = 6 * rows
    qv_grad = vector[at : at + qv_bias.shape[0]]
    at += qv_bias.shape[0]
    fc_bias_grad = vector[at : at + units]
    qkv_got, out_grad = run(7, greet_all, Exchange(qkv_rows), Turn(out_grad_rows, True))
    qkv_grad = (
        widened(fill(qkv_rows, qkv_got, s))
        .reshape(n, rows, 3, wide)
        .transpose(1, 2, 0, 3)
        .reshape(rows, 3 * D)
    )
    return (
        output,
        grad_stream,
        firsts[0],
        firsts[1],
        qkv_grad,
        qv_grad,
        widened(out_grad),
        firsts[2],
        firsts[3],
        firsts[4],
        fc_grad,
        fc_bias_grad,
        proj_grad,
        firsts[5],
    )


def solution(mesh):
    in_specs = (
        P(("dp", "seq"), None),
        P(("dp", "seq"), None),
        P(("dp", "seq")),
        P(("dp", "seq")),
        P(("dp", "seq"), None),
        P(("dp", "seq")),
        P(("dp", "seq"), None),
        P(("dp", "seq")),
        P(("dp", "seq")),
        P(("dp", "seq")),
        P(("dp", "seq"), None),
        P(("dp", "seq")),
        P(("dp", "seq"), None),
        P(("dp", "seq")),
    )
    out_specs = (
        P(("dp", "seq"), None),
        P(("dp", "seq"), None),
        P(("dp", "seq")),
        P(("dp", "seq")),
        P(("dp", "seq"), None),
        P(("dp", "seq")),
        P(("dp", "seq"), None),
        P(("dp", "seq")),
        P(("dp", "seq")),
        P(("dp", "seq")),
        P(("dp", "seq"), None),
        P(("dp", "seq")),
        P(("dp", "seq"), None),
        P(("dp", "seq")),
    )
    return jax.shard_map(local, mesh=mesh, in_specs=in_specs, out_specs=out_specs, check_vma=False)
```

time: 876 us -> 319 us (0.36)
  waiting for transfers between devices: 629 us -> 0 us
  Pallas kernels: 0 us -> 228 us
  blocking collectives: 105 us -> 0 us
  matrix products: 62.5 us -> 33.8 us
  other arithmetic: 14 us -> 29.3 us
  local copies, waits for them, and re-layouts: 39.6 us -> 25.4 us
  between operations: 15 us -> 1.42 us
  starting transfers between devices: 8.88 us -> 0 us
    reduce_scatter x6 -> x0, waiting for transfers between devices: 366 us -> none  [the longest x1 160 us: local(): lax.psum_scatter(d_qkv_weight, ('dp', 'seq'), scatter_dimension=0, tiled=...]
    pallas_call x0 -> x8, Pallas kernels: none -> 228 us  [the longest x7 165 us: run(): pl.pallas_call(kernel, out_shape=[jax.ShapeDtypeStruct(o.shape, o.dtype)...]
    all_gather x8 -> x0, waiting for transfers between devices: 210 us -> none  [the longest x1 52.6 us: local(): lax.all_gather(out_weight, ('dp', 'seq'), axis=0, tiled=True)]
    unnamed x3 -> x0, blocking collectives: 95.5 us -> none
    unnamed x18 -> x0, waiting for transfers between devices: 38.4 us -> none
    dot_general x12, matrix products: 45.8 us -> 23.9 us  [matmul(): return jnp.dot(left, right, preferred_element_type=jnp.float32)]
    unnamed x60 -> x93, local copies, waits for them, and re-layouts: 20.3 us -> 4.11 us
    all_to_all x2 -> x0, waiting for transfers between devices: 15.9 us -> none  [the longest x1 15.9 us: local(): lax.all_to_all(fc_split, 'seq', split_axis=2, concat_axis=0, tiled=True)]
  transfers between devices with their start and end apart: 18 -> 0, of which waited for: 17 -> 0; matrix products, arithmetic and copies ran while one was open for 8% -> 0% of each run, Pallas kernels for 0% -> 0%
where the time goes in v1:
time: 319 us; the launch traced here: 318 us
  Pallas kernels  228 us (71%)
  matrix products  33.8 us (11%)
  other arithmetic  29.3 us (9%)
  local copies, waits for them, and re-layouts  25.4 us (8%)
    pallas_call x7, Pallas kernels, run(): pl.pallas_call(kernel, out_shape=[jax.ShapeDtypeStruct(o.shape, o.dtype)...  165 us
    pallas_call x1, Pallas kernels, gather_inputs(): pl.pallas_call(kernel, out_shape=[grown(block_input, n), grown(cotangent,...  63.2 us
    dot_general x12, matrix products, matmul(): return jnp.dot(left, right, preferred_element_type=jnp.float32)  23.9 us
    convert_element_type x11, other arithmetic, halved(): return values.astype(jnp.bfloat16)  13.4 us

profile of v1, /device:TPU:0, one launch (start us, length us, event | category | flops | bytes accessed | tf_op | source)
XLA Modules:
  0.0 318.4 jit_solution(11782777338338597402)
XLA Ops:
  0.7 5.4 %concatenate.12 = bf16[384]{0:T(512)(128)(2,1)S(1)} concatenate(bf16[32]{0:T(256)(128)(2,1)} %param.16, bf16[32]{0:T(256)(128)(2,1)} %param.17, bf16[32]{0:T(256)(128)(2,1)} %param.21, bf16[32]{0:T(256)(128)(2,1)} %param.22, bf16[32]{0:T(256)(128)(2,1)} %param.23, bf16[32]{0:T(256)(128)(2,1)} %param.27, bf16[64]{0:T(256)(128)(2,1)} %param.19, bf16[128]{0:T(256)(128)(2,1)} %param.25), dimensions={0} | concatenate | bytes 1536 | tf_op jit(solution)/shard_map/concatenate | solution.py:525
  9.9 63.2 %shard_map.245 = (bf16[4,128,1024]{2,1,0:T(8,128)(2,1)}, bf16[4,128,1024]{2,1,0:T(8,128)(2,1)}, bf16[8,4,32,1920]{3,2,1,0:T(8,128)(2,1)}, bf16[8,32,1024]{2,1,0:T(8,128)(2,1)}, bf16[8,128,1024]{2,1,0:T(8,128)(2,1)}) custom-call(bf16[128,1024]{1,0:T(8,128)(2,1)} %x_in.1, bf16[128,1024]{1,0:T(8,128)(2,1)} %g_in.1, ...), custom_call_target="tpu_custom_call" | custom-call | tf_op jit(solution)/shard_map/pallas_call | solution.py:466
  74.6 1.6 multiply_reduce_fusion
  78.5 2.8 fusion.31
  81.9 4.5 %fusion.2 = f32[4,512,512]{1,2,0:T(8,128)} fusion(pred[512,512]{0,1:T(8,128)(4,1)S(1)} %iota_compare_fusion, bf16[4,512,64]{1,2,0:T(8,128)(2,1)S(1)} %bitcast.242, bf16[4,512,64]{1,2,0:T(8,128)(2,1)S(1)} %bitcast.244), kind=kOutput, calls=%fused_computation.3 | convolution fusion | flops 273680896 | bytes 4980736 | tf_op jit(solution)/shard_map/reduce_sum | solution.py:580
  86.4 2.7 convolution_convert_fusion.7
  91.3 25.2 %shard_map.246 = bf16[4,128,1024]{2,1,0:T(8,128)(2,1)} custom-call(bf16[4,128,1024]{2,1,0:T(8,128)(2,1)} %bitcast.203), custom_call_target="tpu_custom_call" | custom-call | tf_op jit(solution)/shard_map/pallas_call | solution.py:342
  119.2 20.7 %shard_map.247 = bf16[4,128,1024]{2,1,0:T(8,128)(2,1)} custom-call(bf16[128,1024]{1,0:T(8,128)(2,1)} %add_convert_fusion.1.refs_0_), custom_call_target="tpu_custom_call" | custom-call | tf_op jit(solution)/shard_map/pallas_call | solution.py:342
  139.9 3.3 %fusion.24 = f32[512,1024]{1,0:T(8,128)S(1)} fusion(bf16[512,1024]{1,0:T(8,128)(2,1)} %bitcast.238, bf16[1024,1920]{1,0:T(8,128)(2,1)} %bitcast.250), kind=kOutput, calls=%fused_computation.36 | convolution fusion | flops 1073741824 | bytes 5242880 | tf_op jit(solution)/shard_map/dot_general | solution.py:45
  143.2 2.5 convolution_convert_fusion.4
  145.8 2.9 fusion.79
  148.6 1.8 convolution_convert_fusion.1
  153.4 2.3 fusion.27
  158.4 24.9 %shard_map.248 = bf16[4,128,1024]{2,1,0:T(8,128)(2,1)} custom-call(bf16[4,128,1024]{2,1,0:T(8,128)(2,1)} %bitcast.210), custom_call_target="tpu_custom_call" | custom-call | tf_op jit(solution)/shard_map/pallas_call | solution.py:342
  183.3 1.7 multiply_reduce_fusion.1
  186.3 22.0 %shard_map.249 = (bf16[4,128,1024]{2,1,0:T(8,128)(2,1)}, bf16[4,128,1024]{2,1,0:T(8,128)(2,1)}, bf16[4,128,1024]{2,1,0:T(8,128)(2,1)}) custom-call(bf16[128,1024]{1,0:T(8,128)(2,1)} %fusion.77.refs_0_, bf16[2,4,128,1024]{3,2,1,0:T(8,128)(2,1)} %bitcast.200, bf16[2,4,128,1024]{3,2,1,0:T(8,128)(2,1)} %bitcast.201), custom_call_target="tpu_custom_call" | custom-call | tf_op jit(solution)/shard_map/pallas_call | solution.py:342
  208.3 2.7 fusion.13.refs_2_
  218.1 3.6 %convolution_convert_fusion.3 = bf16[512,1024]{1,0:T(8,128)(2,1)} fusion(bf16[1024,1920]{1,0:T(8,128)(2,1)} %bitcast.251, f32[512,256]{0,1:T(8,128)S(1)} %bitcast.218, f32[512,256]{0,1:T(8,128)S(1)} %bitcast.227, f32[512,256]{0,1:T(8,128)S(1)} %bitcast.230), kind=kOutput, calls=%fused_computation.42 | convolution fusion | flops 808189952 | bytes 4194304 | tf_op jit(solution)/shard_map/dot_general | solution.py:45
  224.4 25.6 %shard_map.250 = (bf16[4,128,1024]{2,1,0:T(8,128)(2,1)}, bf16[4,128,1024]{2,1,0:T(8,128)(2,1)}, bf16[4,128,1024]{2,1,0:T(8,128)(2,1)}, bf16[4,128,768]{2,1,0:T(8,128)(2,1)}, bf16[4,32,1024]{2,1,0:T(8,128)(2,1)}) custom-call(bf16[4,128,1024]{2,1,0:T(8,128)(2,1)} %bitcast.206, bf16[4,128,1024]{2,1,0:T(8,128)(2,1)} %fusion.14.refs_1_, ...), custom_call_target="tpu_custom_call" | custom-call | tf_op jit(solution)/shard_map/pallas_call | solution.py:342
  250.0 2.5 add_bitcast_fusion
  259.7 35.4 %shard_map.251 = (bf16[4,128,768]{2,1,0:T(8,128)(2,1)}, bf16[4,32,1024]{2,1,0:T(8,128)(2,1)}, bf16[4,32,1024]{2,1,0:T(8,128)(2,1)}, f32[32,3,128]{2,1,0:T(4,128)}, bf16[4,128,1024]{2,1,0:T(8,128)(2,1)}) custom-call(bf16[4,128,768]{2,1,0:T(8,128)(2,1)} %fusion.26.refs_0_, bf16[4,32,1024]{2,1,0:T(8,128)(2,1)} %fusion.57.refs_1_, ...), custom_call_target="tpu_custom_call" | custom-call | tf_op jit(solution)/shard_map/pallas_call | solution.py:342
  295.2 1.7 fusion.68.refs_1_
  297.0 2.1 add_convert_fusion.2
  302.1 11.5 %shard_map.252 = (bf16[4,32,768]{2,1,0:T(8,128)(2,1)}, bf16[32,1024]{1,0:T(8,128)(2,1)}) custom-call(bf16[4,32,768]{2,1,0:T(8,128)(2,1)} %bitcast.235, bf16[32,1024]{1,0:T(8,128)(2,1)} %fusion.68.refs_1_), custom_call_target="tpu_custom_call" | custom-call | tf_op jit(solution)/shard_map/pallas_call | solution.py:342
  (192 shorter events, 44.3 us)
Async XLA Ops:
  73.1 5.0 %copy-start.7 = (bf16[4,128,1024]{2,1,0:T(8,128)(2,1)S(1)}, bf16[4,128,1024]{2,1,0:T(8,128)(2,1)}, u32[]{:S(2)}) copy-start(bf16[4,128,1024]{2,1,0:T(8,128)(2,1)} %get-tuple-element.34) | copy-start | bytes 3145732
  81.6 4.8 %copy-start.33 = (bf16[512,256]{0,1:T(8,128)(2,1)}, bf16[512,256]{0,1:T(8,128)(2,1)S(1)}, u32[]{:S(2)}) copy-start(bf16[512,256]{0,1:T(8,128)(2,1)S(1)} %copy.61) | copy-start | bytes 786436
  81.8 4.6 %copy-start.35 = (bf16[512,256]{0,1:T(8,128)(2,1)}, bf16[512,256]{0,1:T(8,128)(2,1)S(1)}, u32[]{:S(2)}) copy-start(bf16[512,256]{0,1:T(8,128)(2,1)S(1)} %copy.62) | copy-start | bytes 786436
  81.9 4.5 %copy-start.21 = (bf16[512,256]{0,1:T(8,128)(2,1)}, bf16[512,256]{0,1:T(8,128)(2,1)S(1)}, u32[]{:S(2)}) copy-start(bf16[512,256]{0,1:T(8,128)(2,1)S(1)} %copy.63) | copy-start | bytes 786436
  86.4 3.4 %copy-start.23 = (bf16[8,32,1024]{2,1,0:T(8,128)(2,1)S(1)}, bf16[8,32,1024]{2,1,0:T(8,128)(2,1)}, u32[]{:S(2)}) copy-start(bf16[8,32,1024]{2,1,0:T(8,128)(2,1)} %get-tuple-element.36) | copy-start | bytes 1572868
  89.2 27.3 %copy-start.9 = (bf16[128,1024]{1,0:T(8,128)(2,1)S(1)}, bf16[128,1024]{1,0:T(8,128)(2,1)}, u32[]{:S(2)}) copy-start(bf16[128,1024]{1,0:T(8,128)(2,1)} %x_in.1) | copy-start | bytes 786436
  91.3 25.2 %copy-start.6 = (bf16[512,1024]{1,0:T(8,128)(2,1)S(1)}, bf16[512,1024]{1,0:T(8,128)(2,1)}, u32[]{:S(2)}) copy-start(bf16[512,1024]{1,0:T(8,128)(2,1)} %convolution_convert_fusion.5) | copy-start | bytes 3145732
  139.9 3.3 %copy-start.44 = (bf16[8,128,1024]{2,1,0:T(8,128)(2,1)S(1)}, bf16[8,128,1024]{2,1,0:T(8,128)(2,1)}, u32[]{:S(2)}) copy-start(bf16[8,128,1024]{2,1,0:T(8,128)(2,1)} %get-tuple-element.37) | copy-start | bytes 6291460
  150.5 2.9 copy-start.43
  158.4 24.9 %copy-start.15 = (bf16[512,1024]{1,0:T(8,128)(2,1)S(1)}, bf16[512,1024]{1,0:T(8,128)(2,1)}, u32[]{:S(2)}) copy-start(bf16[512,1024]{1,0:T(8,128)(2,1)} %fusion.27) | copy-start | bytes 3145732
  186.3 22.0 %copy-start.2 = (bf16[4,2,128,1024]{3,2,0,1:T(8,128)(2,1)S(1)}, bf16[4,2,128,1024]{3,2,0,1:T(8,128)(2,1)}, u32[]{:S(2)}) copy-start(bf16[4,2,128,1024]{3,2,0,1:T(8,128)(2,1)} %copy.97) | copy-start | bytes 6291460
  218.0 3.8 %copy-start.28 = (bf16[512,1024]{1,0:T(8,128)(2,1)S(1)}, bf16[512,1024]{1,0:T(8,128)(2,1)}, u32[]{:S(2)}) copy-start(bf16[512,1024]{1,0:T(8,128)(2,1)} %copy-done.27) | copy-start | bytes 3145732
  224.4 25.7 %copy-start.5 = (bf16[4,128,1024]{2,1,0:T(8,128)(2,1)S(1)}, bf16[4,128,1024]{2,1,0:T(8,128)(2,1)}, u32[]{:S(2)}) copy-start(bf16[4,128,1024]{2,1,0:T(8,128)(2,1)} %fusion.14.refs_1_) | copy-start | bytes 3145732
  252.5 2.8 copy-start.3
  252.5 2.8 copy-start.37
  257.6 37.7 %copy-start.17 = (bf16[4,32,1024]{2,1,0:T(8,128)(2,1)S(1)}, bf16[4,32,1024]{2,1,0:T(8,128)(2,1)}, u32[]{:S(2)}) copy-start(bf16[4,32,1024]{2,1,0:T(8,128)(2,1)} %fusion.57.refs_1_) | copy-start | bytes 786436
  258.7 38.2 %copy-start.8 = (bf16[4,128,768]{2,1,0:T(8,128)(2,1)S(1)}, bf16[4,128,768]{2,1,0:T(8,128)(2,1)}, u32[]{:S(2)}) copy-start(bf16[4,128,768]{2,1,0:T(8,128)(2,1)} %fusion.26.refs_0_) | copy-start | bytes 2359300
  259.7 39.3 %copy-start.13 = (bf16[512,1024]{1,0:T(8,128)(2,1)S(1)}, bf16[512,1024]{1,0:T(8,128)(2,1)}, u32[]{:S(2)}) copy-start(bf16[512,1024]{1,0:T(8,128)(2,1)} %convolution_convert_fusion.4) | copy-start | bytes 3145732
  295.2 3.9 %copy-start.29 = (bf16[4,128,1024]{2,1,0:T(8,128)(2,1)S(1)}, bf16[4,128,1024]{2,1,0:T(8,128)(2,1)}, u32[]{:S(2)}) copy-start(bf16[4,128,1024]{2,1,0:T(8,128)(2,1)} %get-tuple-element.46) | copy-start | bytes 3145732
  296.9 3.3 %copy-start.38 = (f32[32,3,128]{2,1,0:T(4,128)S(1)}, f32[32,3,128]{2,1,0:T(4,128)}, u32[]{:S(2)}) copy-start(f32[32,3,128]{2,1,0:T(4,128)} %reshape.561.refs_3_) | copy-start | bytes 147460
  296.9 3.3 %copy-start.42 = (f32[32,3,128]{2,1,0:T(4,128)S(1)}, f32[32,3,128]{2,1,0:T(4,128)}, u32[]{:S(2)}) copy-start(f32[32,3,128]{2,1,0:T(4,128)} %get-tuple-element.47) | copy-start | bytes 147460
  299.1 14.5 %copy-start.25 = (bf16[1,128,768]{2,1,0:T(8,128)(2,1)S(1)}, bf16[1,128,768]{2,1,0:T(8,128)(2,1)}, u32[]{:S(2)}) copy-start(bf16[1,128,768]{2,1,0:T(8,128)(2,1)} %add_convert_fusion.2) | copy-start | bytes 589828
  299.1 15.5 %copy-start.18 = (bf16[1,128,1024]{2,1,0:T(8,128)(2,1)S(1)}, bf16[1,128,1024]{2,1,0:T(8,128)(2,1)}, u32[]{:S(2)}) copy-start(bf16[1,128,1024]{2,1,0:T(8,128)(2,1)} %add_convert_fusion) | copy-start | bytes 786436
  299.1 15.5 %copy-start.39 = (bf16[4,32,1024]{2,1,0:T(8,128)(2,1)S(1)}, bf16[4,32,1024]{2,1,0:T(8,128)(2,1)}, u32[]{:S(2)}) copy-start(bf16[4,32,1024]{2,1,0:T(8,128)(2,1)} %get-tuple-element.52) | copy-start | bytes 786436
  (22 other events, 43.2 us)

commit v2 on v1

--- a/solution.py
+++ b/solution.py
@@ -157,16 +157,150 @@
 class Partner(Exchange):
     def __init__(self, value):
         self.operands = (value,)
-        self.outs = (jax.ShapeDtypeStruct(value.shape[1:], value.dtype),)
-        self.sems = (dma(1), dma(1))
+        self.outs = (jax.ShapeDtypeStruct(value.shape[:1] + value.shape[2:], value.dtype),)
+        self.sems = (dma(value.shape[0]), dma(value.shape[0]))
 
     def copies(self, ins, outs, sems):
         dp, s = place()
         return [
             remote(
-                ins[0].at[1 - dp % 2], outs[0], sems[0].at[0], sems[1].at[0], (other_core(dp), s)
+                ins[0].at[k, 1 - dp % 2], outs[0].at[k], sems[0].at[k], sems[1].at[k],
+                (other_core(dp), s),
             )
+            for k in range(self.outs[0].shape[0])
         ]
+
+
+class Spread:
+    def __init__(self, value):
+        dpc, _ = counts()
+        nc = dpc // 2
+        self.operands = (value,)
+        self.outs = (jax.ShapeDtypeStruct((dpc,) + value.shape, value.dtype),)
+        self.sems = (dma(nc), dma(nc), dma(nc), dma(nc), dma(1))
+
+    def to_chips(self, ins, outs, sems):
+        dp, s = place()
+        dpc, _ = counts()
+        nc = dpc // 2
+        return [
+            remote(
+                ins[0], outs[0].at[dp], sems[0].at[k], sems[1].at[k],
+                ((dp // 2 + k) % nc * 2 + dp % 2, s),
+            )
+            for k in range(1, nc)
+        ]
+
+    def to_partner(self, ins, outs, sems, k):
+        dp, s = place()
+        dpc, _ = counts()
+        nc = dpc // 2
+        block = outs[0].at[(dp // 2 - k + nc) % nc * 2 + dp % 2]
+        return remote(
+            ins[0] if k == 0 else block, block, sems[2].at[k], sems[3].at[k], (other_core(dp), s)
+        )
+
+    def start(self, ins, outs, sems):
+        dp, _ = place()
+        for copy in self.to_chips(ins, outs, sems):
+            copy.start()
+        self.to_partner(ins, outs, sems, 0).start()
+        pltpu.make_async_copy(ins[0], outs[0].at[dp], sems[4].at[0]).start()
+
+    def middle(self, ins, outs, sems):
+        dp, s = place()
+        dpc, _ = counts()
+        nc = dpc // 2
+        for k in range(1, nc):
+            slot = (dp // 2 - k + nc) % nc * 2 + dp % 2
+            block = outs[0].at[slot]
+            remote(block, block, sems[0].at[k], sems[1].at[k], (slot, s)).wait_recv()
+            self.to_partner(ins, outs, sems, k).start()
+
+    def close(self, ins, outs, sems):
+        dp, s = place()
+        dpc, _ = counts()
+        nc = dpc // 2
+        for copy in self.to_chips(ins, outs, sems):
+            copy.wait_send()
+        for k in range(nc):
+            self.to_partner(ins, outs, sems, k).wait_send()
+            block = outs[0].at[(dp // 2 - k + nc) % nc * 2 + 1 - dp % 2]
+            remote(block, block, sems[2].at[k], sems[3].at[k], (other_core(dp), s)).wait_recv()
+        pltpu.make_async_copy(ins[0], outs[0].at[dp], sems[4].at[0]).wait()
+
+    def finish(self, ins, outs, sems):
+        self.middle(ins, outs, sems)
+        self.close(ins, outs, sems)
+
+
+class Owners:
+    def __init__(self, value):
+        self.operands = (value,)
+        self.outs = (value,)
+        self.count = value.shape[0] * value.shape[1]
+        self.sems = (dma(self.count), dma(self.count), dma(1))
+
+    def copy(self, ins, outs, sems, k):
+        dp, s = place()
+        dpc, n = counts()
+        chip, z = (dp // 2 + k // n) % (dpc // 2), (s + k % n) % n
+        return remote(
+            ins[0].at[chip, z], outs[0].at[dp // 2, s], sems[0].at[k], sems[1].at[k],
+            (chip * 2 + dp % 2, z),
+        )
+
+    def keep(self, ins, outs, sems):
+        dp, s = place()
+        return pltpu.make_async_copy(ins[0].at[dp // 2, s], outs[0].at[dp // 2, s], sems[2].at[0])
+
+    def start(self, ins, outs, sems):
+        def step(k, carry):
+            self.copy(ins, outs, sems, k).start()
+            return carry
+
+        lax.fori_loop(1, self.count, step, 0)
+        self.keep(ins, outs, sems).start()
+
+    def finish(self, ins, outs, sems):
+        def step(k, carry):
+            self.copy(ins, outs, sems, k).wait()
+            return carry
+
+        lax.fori_loop(1, self.count, step, 0)
+        self.keep(ins, outs, sems).wait()
+
+
+class Blocks:
+    def __init__(self, value):
+        self.operands = (value,)
+        self.outs = (value,)
+        self.sems = (dma(value.shape[0]), dma(value.shape[0]), dma(1))
+
+    def each(self, ins, outs, sems, method):
+        dp, s = place()
+        dpc, n = counts()
+        nc = dpc // 2
+        for k in range(nc):
+            chip = (dp // 2 + k) % nc
+            rank = s * dpc + chip * 2 + dp % 2
+            to_dp, to_s = rank // n, rank % n
+            away = jnp.logical_or(to_dp != dp, to_s != s)
+            source, target = ins[0].at[chip], outs[0].at[dp // 2]
+
+            @pl.when(away)
+            def _():
+                getattr(remote(source, target, sems[0].at[k], sems[1].at[k], (to_dp, to_s)), method)()
+
+            @pl.when(jnp.logical_not(away))
+            def _():
+                getattr(pltpu.make_async_copy(source, target, sems[2].at[0]), method)()
+
+    def start(self, ins, outs, sems):
+        self.each(ins, outs, sems, "start")
+
+    def finish(self, ins, outs, sems):
+        self.each(ins, outs, sems, "wait")
 
 
 class Everyone:
@@ -268,49 +402,6 @@
         for k in range(1, n):
             self.step(ins, outs, sems, k)
         self.close(ins, outs, sems)
-
-
-class Turn:
-    def __init__(self, value, outward):
-        self.outward = outward
-        self.operands = (value,)
-        self.outs = (value,)
-        self.sems = (dma(1), dma(1), dma(1))
-
-    def target(self):
-        dp, s = place()
-        dpc, n = counts()
-        if self.outward:
-            rank = s * dpc + dp
-            return rank // n, rank % n
-        rank = dp * n + s
-        return rank % dpc, rank // dpc
-
-    def away(self):
-        dp, s = place()
-        to_dp, to_s = self.target()
-        return jnp.logical_or(to_dp != dp, to_s != s)
-
-    def copy(self, ins, outs, sems):
-        return remote(ins[0], outs[0], sems[0].at[0], sems[1].at[0], self.target())
-
-    def start(self, ins, outs, sems):
-        @pl.when(self.away())
-        def _():
-            self.copy(ins, outs, sems).start()
-
-        @pl.when(jnp.logical_not(self.away()))
-        def _():
-            pltpu.make_async_copy(ins[0], outs[0], sems[2].at[0]).start()
-
-    def finish(self, ins, outs, sems):
-        @pl.when(self.away())
-        def _():
-            self.copy(ins, outs, sems).wait()
-
-        @pl.when(jnp.logical_not(self.away()))
-        def _():
-            pltpu.make_async_copy(ins[0], outs[0], sems[2].at[0]).wait()
 
 
 def run(number, greet, *tasks):
@@ -349,38 +440,36 @@
     )(*[v for t in tasks for v in t.operands])
 
 
-def gather_inputs(block_input, cotangent, pack, out_rows, proj_rows):
+def gather_inputs(block_input, pack, fc_pack, out_rows):
     dpc, n = counts()
-    nc = dpc // 2
-    tokens, grads = Line(block_input), Line(cotangent)
+    tokens = Line(block_input)
+    spread_out, spread_pack = Spread(out_rows), Spread(pack)
 
     def kernel(
-        x_in, g_in, pack_in, out_in, proj_in, x_all, g_all, pack_all, out_all, proj_all,
-        x_send, x_recv, x_own, g_send, g_recv, g_own, turn_send, turn_recv, local,
-        z_send, z_recv, c_send, c_recv, p_send, p_recv,
+        x_in, pack_in, fc_in, out_in, x_all, pack_all, fc_all, out_all, pack_mid, out_mid,
+        x_send, x_recv, x_own, turn_send, turn_recv, local,
+        z_send, z_recv, f_send, f_recv, *spreads
     ):
         dp, s = place()
-        chip, core = dp // 2, dp % 2
         greet_all()
-        gathered = (proj_all, out_all, pack_all)
         rank = dp * n + s
         to_dp, to_s = rank % dpc, rank // dpc
         home = jnp.logical_and(to_dp == dp, to_s == s)
-        turn = remote(
-            out_in, out_all.at[to_dp], turn_send.at[0], turn_recv.at[0], (to_dp, to_s)
-        )
-        keep_out = pltpu.make_async_copy(out_in, out_all.at[dp], local.at[1])
-        keep_pack = pltpu.make_async_copy(pack_in.at[s], pack_all.at[dp, s], local.at[2])
-        keep_proj = pltpu.make_async_copy(proj_in, proj_all.at[dp], local.at[0])
+        turn = remote(out_in, out_mid, turn_send.at[0], turn_recv.at[0], (to_dp, to_s))
+        keep_out = pltpu.make_async_copy(out_in, out_mid, local.at[0])
+        keep_pack = pltpu.make_async_copy(pack_in.at[s], pack_mid.at[s], local.at[1])
+        keep_fc = pltpu.make_async_copy(fc_in.at[s], fc_all.at[s], local.at[2])
+
+        def shuffle(source, target, send, recv):
+            return [
+                remote(
+                    source.at[(s + k) % n], target.at[s], send.at[k], recv.at[k], (dp, (s + k) % n)
+                )
+                for k in range(n - 1, 0, -1)
+            ]
+
         keep_pack.start()
-        shuffles = [
-            remote(
-                pack_in.at[(s + k) % n], pack_all.at[dp, s], z_send.at[k], z_recv.at[k],
-                (dp, (s + k) % n),
-            )
-            for k in range(n - 1, 0, -1)
-        ]
-        for copy in shuffles:
+        for copy in shuffle(pack_in, pack_mid, z_send, z_recv):
             copy.start()
 
         @pl.when(home)
@@ -391,35 +480,10 @@
         def _():
             turn.start()
 
-        keep_proj.start()
-
-        def to_chips(a, source):
-            return [
-                remote(
-                    source, gathered[a].at[dp], c_send.at[a, k], c_recv.at[a, k],
-                    ((chip + k) % nc * 2 + core, s),
-                )
-                for k in range(1, nc)
-            ]
-
-        def to_partner(a, k, source):
-            slot = (chip - k + nc) % nc * 2 + core
-            return remote(
-                source if source is not None else gathered[a].at[slot],
-                gathered[a].at[slot], p_send.at[a, k], p_recv.at[a, k], (other_core(dp), s),
-            )
-
-        def arrive(a, k):
-            block = gathered[a].at[(chip - k + nc) % nc * 2 + core]
-            remote(
-                block, block, c_send.at[a, k], c_recv.at[a, k], ((chip - k + nc) % nc * 2 + core, s)
-            ).wait_recv()
-
-        sources = (proj_in, out_all.at[dp], pack_all.at[dp])
-        tokens.start((x_in,), (x_all,), (x_send, x_recv, x_own))
-        for copy in to_chips(0, sources[0]):
-            copy.start()
-        to_partner(0, 0, sources[0]).start()
+        token_view = ((x_in,), (x_all,), (x_send, x_recv, x_own))
+        out_view = ((out_mid,), (out_all,), spreads[:5])
+        pack_view = ((pack_mid,), (pack_all,), spreads[5:])
+        tokens.start(*token_view)
 
         @pl.when(home)
         def _():
@@ -429,36 +493,27 @@
         def _():
             turn.wait()
 
+        spread_out.start(*out_view)
         keep_pack.wait()
-        for copy in shuffles:
+        for copy in shuffle(pack_in, pack_mid, z_send, z_recv):
             copy.wait()
-        for a in (1, 2):
-            for copy in to_chips(a, sources[a]):
-                copy.start()
-            to_partner(a, 0, sources[a]).start()
-        for k in range(1, n):
-            tokens.step((x_in,), (x_all,), (x_send, x_recv, x_own), k)
-            if k == 1:
-                grads.start((g_in,), (g_all,), (g_send, g_recv, g_own))
-        for a in range(3):
-            for k in range(1, nc):
-                arrive(a, k)
-                to_partner(a, k, None).start()
-        for k in range(1, n):
-            grads.step((g_in,), (g_all,), (g_send, g_recv, g_own), k)
-        tokens.close((x_in,), (x_all,), (x_send, x_recv, x_own))
-        grads.close((g_in,), (g_all,), (g_send, g_recv, g_own))
-        for a in range(3):
-            for copy in to_chips(a, sources[a]):
-                copy.wait_send()
-            for k in range(nc):
-                slot = (chip - k + nc) % nc * 2 + 1 - core
-                to_partner(a, k, sources[a] if k == 0 else None).wait_send()
-                block = gathered[a].at[slot]
-                remote(
-                    block, block, p_send.at[a, k], p_recv.at[a, k], (other_core(dp), s)
-                ).wait_recv()
-        keep_proj.wait()
+        spread_pack.start(*pack_view)
+        tokens.step(*token_view, 1)
+        keep_fc.start()
+        for copy in shuffle(fc_in, fc_all, f_send, f_recv):
+            copy.start()
+        for k in range(2, n - 1):
+            tokens.step(*token_view, k)
+        spread_out.middle(*out_view)
+        spread_pack.middle(*pack_view)
+        if n > 2:
+            tokens.step(*token_view, n - 1)
+        spread_out.close(*out_view)
+        spread_pack.close(*pack_view)
+        tokens.close(*token_view)
+        keep_fc.wait()
+        for copy in shuffle(fc_in, fc_all, f_send, f_recv):
+            copy.wait()
 
     def grown(value, *lead):
         return jax.ShapeDtypeStruct(lead + value.shape, value.dtype)
@@ -466,17 +521,22 @@
     return pl.pallas_call(
         kernel,
         out_shape=[
-            grown(block_input, n), grown(cotangent, n), grown(pack, dpc), grown(out_rows, dpc),
-            grown(proj_rows, dpc),
+            grown(block_input, n), grown(pack, dpc), grown(fc_pack), grown(out_rows, dpc),
+            grown(pack), grown(out_rows),
         ],
-        in_specs=[pl.BlockSpec(memory_space=pl.ANY)] * 5,
-        out_specs=[pl.BlockSpec(memory_space=pl.ANY)] * 5,
+        in_specs=[pl.BlockSpec(memory_space=pl.ANY)] * 4,
+        out_specs=[pl.BlockSpec(memory_space=pl.ANY)] * 6,
         scratch_shapes=[
-            *tokens.sems, *grads.sems, dma(1), dma(1), dma(3),
-            dma(n), dma(n), dma(3, nc), dma(3, nc), dma(3, nc), dma(3, nc),
+            *tokens.sems, dma(1), dma(1), dma(3),
+            dma(n), dma(n), dma(n), dma(n), *spread_out.sems, *spread_pack.sems,
         ],
         compiler_params=pltpu.CompilerParams(collective_id=0, has_side_effects=True),
-    )(block_input, cotangent, pack, out_rows, proj_rows)
+    )(block_input, pack, fc_pack, out_rows)[:4]
+
+
+def shifted(value, by):
+    _, n = counts()
+    return lax.ppermute(value, "seq", [(i, (i + by) % n) for i in range(n)])
 
 
 def total(own, received, mine):
@@ -522,40 +582,41 @@
     length = n * tok_rows
     score_scale = HD ** (-0.5)
 
-    small = jnp.concatenate(
-        [ln1_gain, ln1_bias, out_bias, ln2_gain, ln2_bias, proj_bias, qv_bias, fc_bias]
-    )
-    margin = -(-small.shape[0] // (rows * 128)) * 128
-    block = jnp.pad(small, (0, rows * margin - small.shape[0])).reshape(rows, margin)
+    fields = (ln1_gain, ln1_bias, out_bias, ln2_gain, ln2_bias, proj_bias, qv_bias, fc_bias)
+    span = -(-max(v.shape[0] for v in fields) // 128) * 128
+    lines = -(-len(fields) // rows) * rows
+    margin = lines // rows * span
+    block = jnp.concatenate([jnp.pad(v[None], ((0, 0), (0, span - v.shape[0]))) for v in fields])
+    block = jnp.pad(block, ((0, lines - len(fields)), (0, 0))).reshape(rows, margin)
     pack = jnp.concatenate(
         [
             qkv_weight.reshape(rows, 3, n, wide).transpose(2, 0, 1, 3).reshape(n, rows, 3 * wide),
-            fc_weight.reshape(rows, dpc, n, units).transpose(2, 0, 1, 3).reshape(n, rows, dpc * units),
             jnp.broadcast_to(block[None], (n, rows, margin)),
         ],
         axis=2,
     )
-    x_all, g_all, pack_all, out_all, proj_all = gather_inputs(
-        block_input, cotangent, pack, out_weight, proj_weight
-    )
+    fc_pack = fc_weight.reshape(rows, dpc, n, units).transpose(2, 0, 1, 3).reshape(n, rows, dpc * units)
+    x_all, pack_all, fc_plane, out_all = gather_inputs(block_input, pack, fc_pack, out_weight)
+    x_all, grad_half = lax.optimization_barrier((x_all, cotangent))
+    grad_all = lax.dynamic_update_index_in_dim(
+        jnp.zeros((n,) + grad_half.shape, grad_half.dtype), grad_half, s, 0
+    )
+    for k in range(1, n):
+        grad_all = lax.dynamic_update_index_in_dim(grad_all, shifted(grad_half, k), (s - k + n) % n, 0)
+    grad_seq = grad_all.reshape(length, D)
     stream_seq = widened(x_all.reshape(length, D))
-    grad_seq = g_all.reshape(length, D)
     pack_rows = pack_all.reshape(D, pack.shape[2])
     qkv_cols = pack_rows[:, : 3 * wide]
-    fc_cols = pack_rows[:, 3 * wide : 3 * wide + dpc * units]
     out_rows = out_all.reshape(wide, D)
-    proj_rows = proj_all.reshape(dpc * units, D)
-    smalls = pack_rows[:, 3 * wide + dpc * units :].reshape(ranks, rows * margin)
+    smalls = pack_rows[:, 3 * wide :].reshape(ranks, lines, span)
     gain_one, bias_one, out_bias_full, gain_two, bias_two, proj_bias_full = (
-        widened(smalls[:, i * rows : (i + 1) * rows].reshape(D)) for i in range(6)
-    )
-    at = 6 * rows
-    qv_full = smalls[:, at : at + qv_bias.shape[0]].reshape(2, n, wide)
+        widened(smalls[:, i, :rows].reshape(D)) for i in range(6)
+    )
+    qv_full = smalls[:, 6, : qv_bias.shape[0]].reshape(2, n, wide)
     qv_own = widened(lax.dynamic_index_in_dim(qv_full, s, 1, keepdims=False))
-    at += qv_bias.shape[0]
     fc_bias_cols = widened(
         lax.dynamic_index_in_dim(
-            smalls[:, at : at + units].reshape(dpc, n, units), s, 1, keepdims=False
+            smalls[:, 7, :units].reshape(dpc, n, units), s, 1, keepdims=False
         ).reshape(dpc * units)
     )
 
@@ -586,11 +647,13 @@
     )
     attended = by_token(attended_heads)
     mixed = halved(matmul(attended, out_rows)).reshape(n, tok_rows, D)
-    (mixed_got,) = run(1, greet_seq, Exchange(mixed))
+    mixed_got, fc_all = run(1, greet_near, Exchange(mixed), Spread(fc_plane))
+    fc_cols = fc_all.reshape(D, dpc * units)
     stream = widened(block_input)
     middle = stream + total(mixed, mixed_got, s) + out_bias_full
     normed_two = halved(layer_norm(middle, gain_two, bias_two))
-    (normed_all,) = run(2, greet_seq, Line(normed_two))
+    normed_all, proj_all = run(2, greet_near, Line(normed_two), Spread(proj_weight))
+    proj_rows = proj_all.reshape(dpc * units, D)
     normed_seq = normed_all.reshape(length, D)
     grad_out = widened(cotangent)
     d_proj_bias = jnp.sum(grad_out, axis=0)
@@ -605,7 +668,7 @@
     ff_part = halved(matmul(hidden, proj_rows)).reshape(n, tok_rows, D)
 
     def by_core(values):
-        return halved(values).reshape(nc, 2, -1, values.shape[-1]).transpose(1, 0, 2, 3)
+        return halved(values).reshape(nc, 2, -1, values.shape[-1])
 
     d_proj = by_core(matmul(hidden.T, grad_seq))
     d_fc = by_core(matmul(normed_seq.T, pre_half))
@@ -619,9 +682,14 @@
     )
 
     def pair(own, received):
-        kept = lax.dynamic_index_in_dim(own, core, 0, keepdims=False)
+        kept = lax.dynamic_index_in_dim(own, core, 1, keepdims=False)
         return halved(widened(kept) + widened(received))
 
+    middle_all, ff_part = lax.optimization_barrier((middle_all, ff_part))
+    ff_sum = widened(lax.dynamic_index_in_dim(ff_part, s, 0, keepdims=False))
+    for k in range(1, n):
+        slot = lax.dynamic_index_in_dim(ff_part, (s + k) % n, 0, keepdims=False)
+        ff_sum = ff_sum + widened(shifted(slot, k))
     d_proj, d_fc = pair(d_proj, d_proj_got), pair(d_fc, d_fc_got)
     middle_half = middle_all.reshape(length, D)
     d_out = by_core(matmul(attended.T, middle_half))
@@ -668,31 +736,30 @@
     )
     used = vectors.shape[1]
     vectors = jnp.pad(vectors, ((0, 0), (0, -used % 128))).reshape(ranks, -1, 128)
-    d_qkv_parts, d_out_parts, fc_got, vectors_got, ff_got = run(
-        6, greet_all, Plane(d_qkv), Plane(d_out), Exchange(fc_rows), Everyone(vectors), Exchange(ff_part)
-    )
-    output = middle + total(ff_part, ff_got, s) + proj_bias_full
+    d_qkv = d_qkv.reshape(nc, n, rows, 3 * wide)
+    d_qkv_parts, d_out_parts, fc_got, vectors_got = run(
+        6, greet_all, Owners(d_qkv), Blocks(d_out), Exchange(fc_rows), Everyone(vectors)
+    )
+    output = middle + ff_sum + proj_bias_full
     fc_grad = (
         widened(fill(fc_rows, fc_got, s))
         .reshape(n, rows, dpc, units)
         .transpose(1, 2, 0, 3)
         .reshape(rows, FF)
     )
-    qkv_rows = halved(total(d_qkv, d_qkv_parts, chip)).reshape(n, rows, 3 * wide)
-    out_grad_rows = halved(total(d_out, d_out_parts, chip))
     vector = jnp.sum(fill(vectors, vectors_got, dp * n + s), axis=0).reshape(-1)
     firsts = [vector[i * rows : (i + 1) * rows] for i in range(6)]
     at = 6 * rows
     qv_grad = vector[at : at + qv_bias.shape[0]]
     at += qv_bias.shape[0]
     fc_bias_grad = vector[at : at + units]
-    qkv_got, out_grad = run(7, greet_all, Exchange(qkv_rows), Turn(out_grad_rows, True))
     qkv_grad = (
-        widened(fill(qkv_rows, qkv_got, s))
+        jnp.sum(widened(d_qkv_parts), axis=0)
         .reshape(n, rows, 3, wide)
         .transpose(1, 2, 0, 3)
         .reshape(rows, 3 * D)
     )
+    out_grad = jnp.sum(widened(d_out_parts), axis=0)
     return (
         output,
         grad_stream,
@@ -700,7 +767,7 @@
         firsts[1],
         qkv_grad,
         qv_grad,
-        widened(out_grad),
+        out_grad,
         firsts[2],
         firsts[3],
         firsts[4],

time: 319 us -> 327 us (1.025)
  matrix products: 33.8 us -> 40.2 us
  starting transfers between devices: 0 us -> 5.9 us
    pallas_call x1, Pallas kernels: 63.2 us -> 39.4 us  [gather_inputs(): pl.pallas_call(kernel, out_shape=[grown(block_input, n), grown(pack, dpc)...]
    pallas_call x7 -> x6, Pallas kernels: 165 us -> 186 us  [run(): pl.pallas_call(kernel, out_shape=[jax.ShapeDtypeStruct(o.shape, o.dtype)...]
    dot_general x12, matrix products: 23.9 us -> 30.3 us  [matmul(): return jnp.dot(left, right, preferred_element_type=jnp.float32)]
    ppermute x0 -> x6, starting transfers between devices: none -> 5.9 us  [shifted(): return lax.ppermute(value, 'seq', [(i, (i + by) % n) for i in range(n)])]
    reshape x9 -> x2, local copies, waits for them, and re-layouts: 6.77 us -> 1.16 us  [local(): qkv_grad = jnp.sum(widened(d_qkv_parts), axis=0).reshape(n, rows, 3, wide...]
    concatenate x1, local copies, waits for them, and re-layouts: 5.43 us -> 0.68 us  [local(): jnp.concatenate([jnp.pad(v[None], ((0, 0), (0, span - v.shape[0]))) for v...]
    pad x0 -> x8, local copies, waits for them, and re-layouts: none -> 4.64 us  [the longest x7 4.63 us: local(): jnp.pad(v[None], ((0, 0), (0, span - v.shape[0])))]
    convert_element_type x11 -> x9, other arithmetic: 13.4 us -> 13.2 us  [halved(): return values.astype(jnp.bfloat16)]
  transfers between devices with their start and end apart: 0 -> 6, of which waited for: 0 -> 0; matrix products, arithmetic and copies ran while one was open for 0% -> 14% of each run, Pallas kernels for 0% -> 42%
where the time goes in v2:
time: 327 us
  Pallas kernels  226 us (69%)
  matrix products  40.2 us (12%)
  other arithmetic  30.8 us (9%)
  local copies, waits for them, and re-layouts  22.7 us (7%)
  starting transfers between devices  5.9 us (2%)
    pallas_call x6, Pallas kernels, run(): pl.pallas_call(kernel, out_shape=[jax.ShapeDtypeStruct(o.shape, o.dtype)...  186 us
    pallas_call x1, Pallas kernels, gather_inputs(): pl.pallas_call(kernel, out_shape=[grown(block_input, n), grown(pack, dpc)...  39.4 us
    dot_general x12, matrix products, matmul(): return jnp.dot(left, right, preferred_element_type=jnp.float32)  30.3 us
    convert_element_type x9, other arithmetic, halved(): return values.astype(jnp.bfloat16)  13.2 us
  transfers between devices with their start and end apart: 6, of which 0 were waited for; matrix products, arithmetic and copies ran while one was open for 14% of the time, Pallas kernels for 42%

profile of v2, /device:TPU:0, one launch (start us, length us, event | category | flops | bytes accessed | tf_op | source)
XLA Modules:
  0.0 326.6 jit_solution(2995315011599519445)
XLA Ops:
  10.1 39.4 %shard_map.245 = (bf16[4,128,1024]{2,1,0:T(8,128)(2,1)}, bf16[8,4,32,896]{3,2,1,0:T(8,128)(2,1)}, bf16[4,32,1024]{2,1,0:T(8,128)(2,1)}, bf16[8,32,1024]{2,1,0:T(...) custom-call(bf16[128,1024]{1,0:T(8,128)(2,1)} %x_in.1, ...), custom_call_target="tpu_custom_call" | custom-call | tf_op jit(solution)/shard_map/pallas_call | solution.py:521
  59.6 4.4 %fusion.2 = f32[4,512,512]{1,2,0:T(8,128)} fusion(pred[512,512]{0,1:T(8,128)(4,1)S(1)} %copy-done.23, bf16[4,512,64]{1,2,0:T(8,128)(2,1)S(1)} %bitcast.253, bf16[4,512,64]{1,2,0:T(8,128)(2,1)S(1)} %bitcast.255), kind=kOutput, calls=%fused_computation.3 | convolution fusion | flops 273680896 | bytes 4980736 | tf_op jit(solution)/shard_map/reduce_sum | solution.py:641
  64.1 2.7 convolution_convert_fusion.8
  68.3 31.9 %shard_map.246 = (bf16[4,128,1024]{2,1,0:T(8,128)(2,1)}, bf16[8,4,32,1024]{3,2,1,0:T(8,128)(2,1)}) custom-call(bf16[4,128,1024]{2,1,0:T(8,128)(2,1)} %bitcast.211, bf16[4,32,1024]{2,1,0:T(8,128)(2,1)} %get-tuple-element.42.refs_1_), custom_call_target="tpu_custom_call" | custom-call | tf_op jit(solution)/shard_map/pallas_call | solution.py:433
  103.3 26.7 %shard_map.247 = (bf16[4,128,1024]{2,1,0:T(8,128)(2,1)}, bf16[8,128,1024]{2,1,0:T(8,128)(2,1)}) custom-call(bf16[128,1024]{1,0:T(8,128)(2,1)} %add_convert_fusion.1.refs_0_, bf16[128,1024]{1,0:T(8,128)(2,1)} %refs_1_.1), custom_call_target="tpu_custom_call" | custom-call | tf_op jit(solution)/shard_map/pallas_call | solution.py:433
  130.0 3.3 %fusion.89 = f32[512,1024]{1,0:T(8,128)S(1)} fusion(bf16[512,1024]{1,0:T(8,128)(2,1)} %bitcast.280, bf16[1024,1024]{1,0:T(8,128)(2,1)} %bitcast.276), kind=kOutput, calls=%fused_computation.179 | convolution fusion | flops 1073741824 | bytes 5242880 | tf_op jit(solution)/shard_map/dot_general | solution.py:45
  133.3 2.5 convolution_convert_fusion.4
  137.4 5.4 %fusion.78 = (f32[1024]{0:T(1024)S(1)}, bf16[512,1024]{1,0:T(8,128)(2,1)S(1)}) fusion(f32[512,1024]{1,0:T(8,128)} %copy-done.29, f32[1024]{0:T(1024)S(1)} %bitcast.271, bf16[512,1024]{1,0:T(8,128)(2,1)S(1)} %bitcast.250, bf16[1024,1024]{1,0:T(8,128)(2,1)} %bitcast.278), kind=kOutput, calls=%fused_computation.172 | convolution fusion | flops 1087372288 | bytes 6299648 | tf_op jit(solution)/shard_map/dot_general | solution.py:45
  142.8 3.0 convolution_convert_fusion.1
  145.8 2.4 convolution_convert_fusion.5
  148.2 2.6 convolution_convert_fusion
  150.8 26.7 %shard_map.248 = bf16[4,128,1024]{2,1,0:T(8,128)(2,1)} custom-call(bf16[4,128,1024]{2,1,0:T(8,128)(2,1)} %bitcast.221), custom_call_target="tpu_custom_call" | custom-call | tf_op jit(solution)/shard_map/pallas_call | solution.py:433
  180.4 21.6 %shard_map.249 = (bf16[4,128,1024]{2,1,0:T(8,128)(2,1)}, bf16[4,128,1024]{2,1,0:T(8,128)(2,1)}, bf16[4,128,1024]{2,1,0:T(8,128)(2,1)}) custom-call(bf16[128,1024]{1,0:T(8,128)(2,1)} %fusion.75.refs_0_, bf16[4,2,128,1024]{3,2,1,0:T(8,128)(2,1)} %bitcast.212, bf16[4,2,128,1024]{3,2,1,0:T(8,128)(2,1)} %bitcast.214), custom_call_target="tpu_custom_call" | custom-call | tf_op jit(solution)/shard_map/pallas_call | solution.py:433
  203.9 2.5 convolution_convert_fusion.7
  210.4 2.1 convolution_convert_fusion.3
  212.7 2.2 convolution_convert_fusion.2
  215.0 3.2 fusion.13.refs_2_
  221.8 3.8 %collective-permute-start.5 = (bf16[128,1024]{1,0:T(8,128)(2,1)}, bf16[128,1024]{1,0:T(8,128)(2,1)}, u32[]{:S(2)}, u32[]{:S(2)}) collective-permute-start(bf16[128,1024]{1,0:T(8,128)(2,1)} %get-tuple-element.89), channel_id=1, source_target_pairs={{0,3},{1,0},{2,1},{3,2},{4,7},{5,4},{6,5},{7,6},{8,11},{9,8},{10,9... | collective-permute-start | bytes 786440 | tf_op jit(solution)/shard_map/ppermute | solution.py:539
  225.6 42.7 %shard_map.250 = (bf16[4,128,1024]{2,1,0:T(8,128)(2,1)}, bf16[4,128,1024]{2,1,0:T(8,128)(2,1)}, bf16[4,128,1024]{2,1,0:T(8,128)(2,1)}, bf16[4,128,768]{2,1,0:T(8,128)(2,1)}, bf16[4,32,1024]{2,1,0:T(8,128)(2,1)}) custom-call(bf16[4,128,1024]{2,1,0:T(8,128)(2,1)} %bitcast.216, bf16[4,128,1024]{2,1,0:T(8,128)(2,1)} %fusion.14.refs_1_, ...), custom_call_target="tpu_custom_call" | custom-call | tf_op jit(solution)/shard_map/pallas_call | solution.py:433
  270.2 2.2 fusion.22
  275.6 2.3 add_convert_fusion
  277.9 36.5 %shard_map.251 = (bf16[4,4,32,768]{3,2,1,0:T(8,128)(2,1)}, bf16[4,32,1024]{2,1,0:T(8,128)(2,1)}, bf16[4,32,1024]{2,1,0:T(8,128)(2,1)}, f32[32,3,128]{2,1,0:T(4,128)}) custom-call(bf16[4,4,32,768]{3,2,1,0:T(8,128)(2,1)} %bitcast.226, bf16[4,32,1024]{2,1,0:T(8,128)(2,1)} %fusion.42.refs_1_, bf16[4,32,1024]{2,1,0:T(8,128)(2,1)} %bitcast.227, ...), custom_call_target="tpu_custom_call" | custom-call | tf_op jit(solution)/shard_map/pallas_call | solution.py:433
  322.0 2.3 add_bitcast_fusion
  324.4 2.2 fusion.49
  (180 shorter events, 50.5 us)
Async XLA Ops:
  6.0 43.6 %copy-start.10 = (bf16[128,1024]{1,0:T(8,128)(2,1)S(1)}, bf16[128,1024]{1,0:T(8,128)(2,1)}, u32[]{:S(2)}) copy-start(bf16[128,1024]{1,0:T(8,128)(2,1)} %param.15) | copy-start | bytes 786436
  49.6 5.7 %copy-start.3 = (bf16[4,128,1024]{2,1,0:T(8,128)(2,1)S(1)}, bf16[4,128,1024]{2,1,0:T(8,128)(2,1)}, u32[]{:S(2)}) copy-start(bf16[4,128,1024]{2,1,0:T(8,128)(2,1)} %get-tuple-element.39) | copy-start | bytes 3145732
  49.6 87.7 %collective-permute-start.2 = (bf16[128,1024]{1,0:T(8,128)(2,1)S(1)}, bf16[128,1024]{1,0:T(8,128)(2,1)S(1)}, u32[]{:S(2)}, u32[]{:S(2)}) collective-permute-start(bf16[128,1024]{1,0:T(8,128)(2,1)S(1)} %copy-done.10), channel_id=1, source_target_pairs={{0,3},{1,0},{2,1},{3,2},{4,7},{5,4},{6,5},{7,6},{8,11},{9,8},{10,9... | collective-permute-start | bytes 786440 | tf_op jit(solution)/shard_map/ppermute | solution.py:539
  49.6 87.6 %collective-permute-start.1 = (bf16[128,1024]{1,0:T(8,128)(2,1)S(1)}, bf16[128,1024]{1,0:T(8,128)(2,1)S(1)}, u32[]{:S(2)}, u32[]{:S(2)}) collective-permute-start(bf16[128,1024]{1,0:T(8,128)(2,1)S(1)} %copy-done.10), channel_id=1, source_target_pairs={{0,2},{1,3},{2,0},{3,1},{4,6},{5,7},{6,4},{7,5},{8,10},{9,11},{10,... | collective-permute-start | bytes 786440 | tf_op jit(solution)/shard_map/ppermute | solution.py:539
  50.6 85.7 %collective-permute-start = (bf16[128,1024]{1,0:T(8,128)(2,1)S(1)}, bf16[128,1024]{1,0:T(8,128)(2,1)}, u32[]{:S(2)}, u32[]{:S(2)}) collective-permute-start(bf16[128,1024]{1,0:T(8,128)(2,1)S(1)} %copy-done.10), channel_id=1, source_target_pairs={{0,1},{1,2},{2,3},{3,0},{4,5},{5,6},{6,7},{7,4},{8,9},{9,10},{10,1... | collective-permute-start | bytes 786440 | tf_op jit(solution)/shard_map/ppermute | solution.py:539
  59.1 4.9 %copy-start.18 = (bf16[512,256]{0,1:T(8,128)(2,1)}, bf16[512,256]{0,1:T(8,128)(2,1)S(1)}, u32[]{:S(2)}) copy-start(bf16[512,256]{0,1:T(8,128)(2,1)S(1)} %copy.59) | copy-start | bytes 786436
  66.8 33.4 %copy-start.4 = (bf16[128,1024]{1,0:T(8,128)(2,1)S(1)}, bf16[128,1024]{1,0:T(8,128)(2,1)}, u32[]{:S(2)}) copy-start(bf16[128,1024]{1,0:T(8,128)(2,1)} %x_in.1) | copy-start | bytes 786436
  130.0 3.3 %copy-start.27 = (bf16[8,128,1024]{2,1,0:T(8,128)(2,1)S(1)}, bf16[8,128,1024]{2,1,0:T(8,128)(2,1)}, u32[]{:S(2)}) copy-start(bf16[8,128,1024]{2,1,0:T(8,128)(2,1)} %get-tuple-element.47) | copy-start | bytes 6291460
  137.4 5.4 %copy-start.30 = (f32[512,1024]{1,0:T(8,128)S(1)}, f32[512,1024]{1,0:T(8,128)}, u32[]{:S(2)}) copy-start(f32[512,1024]{1,0:T(8,128)} %copy-done.29) | copy-start | bytes 6291460
  142.8 3.0 copy-start.26
  150.8 26.7 %copy-start.7 = (bf16[512,1024]{1,0:T(8,128)(2,1)S(1)}, bf16[512,1024]{1,0:T(8,128)(2,1)}, u32[]{:S(2)}) copy-start(bf16[512,1024]{1,0:T(8,128)(2,1)} %convolution_convert_fusion.5) | copy-start | bytes 3145732
  180.4 21.6 %copy-start.13 = (bf16[8,32,1024]{2,1,0:T(8,128)(2,1)S(1)}, bf16[8,32,1024]{2,1,0:T(8,128)(2,1)}, u32[]{:S(2)}) copy-start(bf16[8,32,1024]{2,1,0:T(8,128)(2,1)} %get-tuple-element.41) | copy-start | bytes 1572868
  202.0 4.4 %copy-start = (f32[4,512,512]{1,2,0:T(8,128)S(1)}, f32[4,512,512]{1,2,0:T(8,128)}, u32[]{:S(2)}) copy-start(f32[4,512,512]{1,2,0:T(8,128)} %fusion.2) | copy-start | bytes 12582916
  214.9 3.3 %copy-start.5 = (bf16[1024,1024]{1,0:T(8,128)(2,1)S(1)}, bf16[1024,1024]{1,0:T(8,128)(2,1)}, u32[]{:S(2)}) copy-start(bf16[1024,1024]{1,0:T(8,128)(2,1)} %convolution_convert_fusion.1) | copy-start | bytes 6291460
  215.0 3.2 copy-start.17
  221.8 102.6 %collective-permute-start.3 = (bf16[128,1024]{1,0:T(8,128)(2,1)}, bf16[128,1024]{1,0:T(8,128)(2,1)}, u32[]{:S(2)}, u32[]{:S(2)}) collective-permute-start(bf16[128,1024]{1,0:T(8,128)(2,1)} %get-tuple-element.88), channel_id=1, source_target_pairs={{0,1},{1,2},{2,3},{3,0},{4,5},{5,6},{6,7},{7,4},{8,9},{9,10},{10,1... | collective-permute-start | bytes 786440 | tf_op jit(solution)/shard_map/ppermute | solution.py:539
  221.8 102.6 %collective-permute-start.5 = (bf16[128,1024]{1,0:T(8,128)(2,1)}, bf16[128,1024]{1,0:T(8,128)(2,1)}, u32[]{:S(2)}, u32[]{:S(2)}) collective-permute-start(bf16[128,1024]{1,0:T(8,128)(2,1)} %get-tuple-element.89), channel_id=1, source_target_pairs={{0,3},{1,0},{2,1},{3,2},{4,7},{5,4},{6,5},{7,6},{8,11},{9,8},{10,9... | collective-permute-start | bytes 786440 | tf_op jit(solution)/shard_map/ppermute | solution.py:539
  225.6 98.8 %collective-permute-start.4 = (bf16[128,1024]{1,0:T(8,128)(2,1)}, bf16[128,1024]{1,0:T(8,128)(2,1)}, u32[]{:S(2)}, u32[]{:S(2)}) collective-permute-start(bf16[128,1024]{1,0:T(8,128)(2,1)} %get-tuple-element.90), channel_id=1, source_target_pairs={{0,2},{1,3},{2,0},{3,1},{4,6},{5,7},{6,4},{7,5},{8,10},{9,11},{10,... | collective-permute-start | bytes 786440 | tf_op jit(solution)/shard_map/ppermute | solution.py:539
  225.6 42.7 %copy-start.9 = (bf16[256,1024]{1,0:T(8,128)(2,1)S(1)}, bf16[256,1024]{1,0:T(8,128)(2,1)}, u32[]{:S(2)}) copy-start(bf16[256,1024]{1,0:T(8,128)(2,1)} %convolution_convert_fusion.7) | copy-start | bytes 1572868
  225.6 44.6 %copy-start.8 = (bf16[1024,768]{1,0:T(8,128)(2,1)S(1)}, bf16[1024,768]{1,0:T(8,128)(2,1)}, u32[]{:S(2)}) copy-start(bf16[1024,768]{1,0:T(8,128)(2,1)} %convolution_convert_fusion.2) | copy-start | bytes 4718596
  268.3 4.1 %copy-start.6 = (bf16[512,1024]{1,0:T(8,128)(2,1)S(1)}, bf16[512,1024]{1,0:T(8,128)(2,1)}, u32[]{:S(2)}) copy-start(bf16[512,1024]{1,0:T(8,128)(2,1)} %convolution_convert_fusion.3) | copy-start | bytes 3145732
  268.3 4.1 %copy-start.14 = (bf16[4,128,1024]{2,1,0:T(8,128)(2,1)S(1)}, bf16[4,128,1024]{2,1,0:T(8,128)(2,1)}, u32[]{:S(2)}) copy-start(bf16[4,128,1024]{2,1,0:T(8,128)(2,1)} %get-tuple-element.53) | copy-start | bytes 3145732
  275.6 38.8 %copy-start.21 = (f32[32,3,128]{2,1,0:T(4,128)S(1)}, f32[32,3,128]{2,1,0:T(4,128)}, u32[]{:S(2)}) copy-start(f32[32,3,128]{2,1,0:T(4,128)} %reshape.484.refs_3_) | copy-start | bytes 147460
  314.4 3.5 %copy-start.20 = (bf16[4,4,32,768]{3,2,1,0:T(8,128)(2,1)S(1)}, bf16[4,4,32,768]{3,2,1,0:T(8,128)(2,1)}, u32[]{:S(2)}) copy-start(bf16[4,4,32,768]{3,2,1,0:T(8,128)(2,1)} %get-tuple-element.58) | copy-start | bytes 2359300
  (13 other events, 23.4 us)
